TPU v7x, 32 devices: a whole 2x2x4 slice. The times are simulated.
32 devices in a mesh: fsdp: 2 (over y), ctx: 4 (over x, core), tp: 4 (over z).
Axes of the slice: x: 2, y: 2, z: 4, core: 2. Of those that a mesh axis runs over, the one named last changes fastest.
Arguments:
- tokens: bfloat16 [8192, 2048], P(('fsdp', 'ctx')), may hold values from -6 to 6
- cotangent: bfloat16 [8192, 2048], P(('fsdp', 'ctx')), may hold values from -6 to 6
- piece_ids: int32 [8192], P(('fsdp', 'ctx')), may hold values from 0 to 32, as said below
- positions: int32 [8192], P(('fsdp', 'ctx')), may hold values from 0 to 12285, as said below
- norm_gain: bfloat16 [2048], replicated, may hold values from 0.5 to 1.5
- norm_shift: bfloat16 [2048], replicated, may hold values from -1.1953125 to 1.1953125
- in_proj: bfloat16 [3, 2048, 2048], P(None, ('fsdp', 'ctx'), 'tp'), may hold values from -0.125 to 0.125
- in_bias: bfloat16 [3, 2048], P(None, 'tp'), may hold values from -0.119628906 to 0.119628906
- out_proj: bfloat16 [2048, 2048], P('tp', ('fsdp', 'ctx')), may hold values from -3 to 3
- up_proj: bfloat16 [2048, 8192], P(('fsdp', 'ctx'), 'tp'), may hold values from -0.125 to 0.125
- up_bias: bfloat16 [8192], P('tp'), may hold values from -3 to 3
- down_proj: bfloat16 [8192, 2048], P('tp', ('fsdp', 'ctx')), may hold values from -0.0625 to 0.0625
- out_bias: bfloat16 [2048], replicated, may hold values from -1.1953125 to 1.1953125
Outputs:
- layer_out: bfloat16 [8192, 2048], P(('fsdp', 'ctx', 'tp'))
- input_grad: bfloat16 [8192, 2048], P(('fsdp', 'ctx', 'tp'))
- gain_grad: float32 [2048], replicated
- shift_grad: float32 [2048], replicated
- inproj_grad: float32 [3, 2048, 2048], P(None, ('fsdp', 'ctx'), 'tp')
- inbias_grad: float32 [3, 2048], P(None, 'tp')
- outproj_grad: float32 [2048, 2048], P('tp', ('fsdp', 'ctx'))
- upproj_grad: float32 [2048, 8192], P(('fsdp', 'ctx'), 'tp')
- upbias_grad: float32 [8192], P('tp')
- downproj_grad: float32 [8192, 2048], P('tp', ('fsdp', 'ctx'))
- outbias_grad: float32 [2048], replicated
Inputs may be any that keep to these rules, and one draw needn't show every extreme that they name: `piece_ids`: each aligned run of 256 rows carries one number: 0 for text, or for a picture piece a number that no other run carries; the last run of all is a picture piece. Within each sequence of 4096 consecutive rows positions start at 0 and rise by 1, 2 or 3 from one row to the next; in the last sequence they rise by 3 throughout.
All inputs are finite; a program needn't handle non-finite values.
Results may differ from a plain program's by a relative error of at most 0.015.
Values may be sent and summed in bfloat16 or wider, within the bound.
A program may use at most 192 MiB of HBM per device.

v0:
```python
import math

import jax
import jax.numpy as jnp
from jax import lax
from jax.sharding import PartitionSpec as P

HD = 64
ROT = 32
LEN = 4096


EPS = 1e-05
NEG = -1e30


def layer_norm(values, scaling, offset):
    center = values - jnp.mean(values, axis=-1, keepdims=True)
    spread = jnp.mean(center * center, axis=-1, keepdims=True)
    return center * lax.rsqrt(spread + EPS) * scaling + offset


def rotary_angles(places):
    frequency = 10000.0 ** (-2.0 * jnp.arange(ROT // 2, dtype=jnp.float32) / ROT)
    return places.astype(jnp.float32)[:, None] * frequency[None, :]


def rotate(values, angles):
    shaped = values.reshape(values.shape[0], -1, HD)
    half_rot = ROT // 2
    lower_half = shaped[..., :half_rot]
    upper_half = shaped[..., half_rot:ROT]
    remainder = shaped[..., ROT:]
    cos_part = jnp.cos(angles)[:, None, :]
    sin_part = jnp.sin(angles)[:, None, :]
    turned = jnp.concatenate(
        [
            lower_half * cos_part - upper_half * sin_part,
            upper_half * cos_part + lower_half * sin_part,
            remainder,
        ],
        axis=-1,
    )
    return turned.reshape(values.shape)


def gelu_tanh(values):
    return jax.nn.gelu(values, approximate=True)


def dot_last(matrix_a, matrix_b):
    return lax.dot_general(
        matrix_a,
        matrix_b,
        (((matrix_a.ndim - 1,), (matrix_b.ndim - 1,)), ((), ())),
        preferred_element_type=jnp.float32,
    )


def dot_first(matrix_a, matrix_b):
    return lax.dot_general(
        matrix_a, matrix_b, (((0,), (0,)), ((), ())), preferred_element_type=jnp.float32
    )


def visible(query_row, query_pos, query_piece, key_row, key_pos, key_piece):
    same_seq = query_row[:, None] // LEN == key_row[None, :] // LEN
    before = key_pos[None, :] <= query_pos[:, None]
    picture = (key_piece[None, :] == query_piece[:, None]) & (query_piece[:, None] > 0)
    return same_seq & (before | picture)


def scores_of(query_vals, key_vals, visible_pairs, score_scale):
    scores = (
        jnp.einsum("qhd,khd->hqk", query_vals, key_vals, preferred_element_type=jnp.float32)
        * score_scale
    )
    return jnp.where(visible_pairs[None], scores, NEG)


def pair_grads(
    query_vals, grad_vals, log_total, delta_row, key_vals, value_vals, visible_pairs, score_scale
):
    scores = scores_of(query_vals, key_vals, visible_pairs, score_scale)
    softmax = jnp.exp(scores - log_total[..., None])
    grad_probs = jnp.einsum(
        "qhd,khd->hqk", grad_vals, value_vals, preferred_element_type=jnp.float32
    )
    grad_scores = (softmax * (grad_probs - delta_row[..., None])).astype(jnp.bfloat16)
    return (softmax.astype(jnp.bfloat16), grad_scores)


def unchanged(states):
    return states


def body(
    tokens,
    cotangent,
    piece_ids,
    positions,
    norm_gain,
    norm_shift,
    in_proj,
    in_bias,
    out_proj,
    up_proj,
    up_bias,
    down_proj,
    out_bias,
):
    length = tokens.shape[0]
    score_scale = 1.0 / math.sqrt(HD)
    width_local = in_bias.shape[1]
    heads_local = width_local // HD
    ctx_count = lax.axis_size("ctx")
    tp_count = lax.axis_size("tp")
    share_rows = length // tp_count
    share_start = lax.axis_index("tp") * share_rows
    query_block = math.gcd(length, 512)
    key_block = math.gcd(length, 1024)
    query_blocks = length // query_block
    whole_rows = length * ctx_count
    key_blocks = whole_rows // key_block
    inproj_all, outproj_all, upproj_all, downproj_all = (
        lax.all_gather(in_proj, ("fsdp", "ctx"), axis=1, tiled=True),
        lax.all_gather(out_proj, ("fsdp", "ctx"), axis=1, tiled=True),
        lax.all_gather(up_proj, ("fsdp", "ctx"), axis=0, tiled=True),
        lax.all_gather(down_proj, ("fsdp", "ctx"), axis=1, tiled=True),
    )
    tokens_full = tokens.astype(jnp.float32)
    gain_full = norm_gain.astype(jnp.float32)
    shift_full = norm_shift.astype(jnp.float32)
    normed = layer_norm(tokens_full, gain_full, shift_full).astype(jnp.bfloat16)
    packed = (
        jnp.einsum("td,jde->jte", normed, inproj_all, preferred_element_type=jnp.float32)
        + in_bias.astype(jnp.float32)[:, None, :]
    )
    angles = rotary_angles(positions)
    queries = rotate(packed[0], angles).astype(jnp.bfloat16)
    keys_local = rotate(packed[1], angles).astype(jnp.bfloat16)
    values_local = packed[2].astype(jnp.bfloat16)
    keys_all, values_all, pieces_all, places_all = (
        lax.all_gather(keys_local, "ctx", axis=0, tiled=True),
        lax.all_gather(values_local, "ctx", axis=0, tiled=True),
        lax.all_gather(piece_ids, "ctx", axis=0, tiled=True),
        lax.all_gather(positions, "ctx", axis=0, tiled=True),
    )
    query_rows = lax.axis_index("ctx") * length + jnp.arange(length, dtype=jnp.int32)
    key_rows = jnp.arange(whole_rows, dtype=jnp.int32)
    query_heads = queries.reshape(query_blocks, query_block, heads_local, HD)
    qrow_blocks = query_rows.reshape(query_blocks, query_block)
    qpos_blocks = positions.reshape(query_blocks, query_block)
    qpiece_blocks = piece_ids.reshape(query_blocks, query_block)
    key_stack = (
        keys_all.reshape(key_blocks, key_block, heads_local, HD),
        values_all.reshape(key_blocks, key_block, heads_local, HD),
        key_rows.reshape(key_blocks, key_block),
        places_all.reshape(key_blocks, key_block),
        pieces_all.reshape(key_blocks, key_block),
    )

    def forward_block(query_args):
        query_vals, query_row, query_pos, query_piece = query_args

        def online_step(carried, key_args):
            key_vals, value_vals, key_row, key_pos, key_piece = key_args
            visible_pairs = visible(query_row, query_pos, query_piece, key_row, key_pos, key_piece)

            def online_update(states):
                running, summed, output = states
                scores = scores_of(query_vals, key_vals, visible_pairs, score_scale)
                newmax = jnp.maximum(running, jnp.max(scores, axis=-1))
                rescale = jnp.exp(running - newmax)
                weights = jnp.exp(scores - newmax[..., None])
                summed = summed * rescale + jnp.sum(weights, axis=-1)
                output = output * jnp.transpose(rescale)[:, :, None] + jnp.einsum(
                    "hqk,khd->qhd",
                    weights.astype(jnp.bfloat16),
                    value_vals,
                    preferred_element_type=jnp.float32,
                )
                return (newmax, summed, output)

            return (lax.cond(jnp.any(visible_pairs), online_update, unchanged, carried), None)

        start_state = (
            jnp.full((heads_local, query_block), NEG, jnp.float32),
            jnp.zeros((heads_local, query_block), jnp.float32),
            jnp.zeros((query_block, heads_local, HD), jnp.float32),
        )
        (running, summed, output), _ = lax.scan(online_step, start_state, key_stack)
        log_total = running + jnp.log(summed)
        return (output / jnp.transpose(summed)[:, :, None], log_total)

    attn_blocks, log_totals = lax.map(
        forward_block, (query_heads, qrow_blocks, qpos_blocks, qpiece_blocks)
    )
    attended = attn_blocks.reshape(length, width_local).astype(jnp.bfloat16)
    upward = jnp.dot(normed, upproj_all, preferred_element_type=jnp.float32) + up_bias.astype(
        jnp.float32
    )
    active = gelu_tanh(upward).astype(jnp.bfloat16)
    branch = lax.psum_scatter(
        (
            jnp.dot(attended, outproj_all, preferred_element_type=jnp.float32)
            + jnp.dot(active, downproj_all, preferred_element_type=jnp.float32)
        ).astype(jnp.bfloat16),
        "tp",
        scatter_dimension=0,
        tiled=True,
    ).astype(jnp.float32)
    token_share = lax.dynamic_slice_in_dim(tokens_full, share_start, share_rows, 0)
    layer_out = (token_share + branch + out_bias.astype(jnp.float32)).astype(jnp.bfloat16)
    inproj_back, outproj_back, upproj_back, downproj_back = (
        lax.all_gather(in_proj, ("fsdp", "ctx"), axis=1, tiled=True),
        lax.all_gather(out_proj, ("fsdp", "ctx"), axis=1, tiled=True),
        lax.all_gather(up_proj, ("fsdp", "ctx"), axis=0, tiled=True),
        lax.all_gather(down_proj, ("fsdp", "ctx"), axis=1, tiled=True),
    )
    outproj_full = dot_first(attended, cotangent)
    downproj_full = dot_first(active, cotangent)
    grad_attended = dot_last(cotangent, outproj_back).astype(jnp.bfloat16)
    grad_active = dot_last(cotangent, downproj_back)
    _, gelu_back = jax.vjp(gelu_tanh, upward)
    grad_upward = gelu_back(grad_active)[0].astype(jnp.bfloat16)
    upproj_full = dot_first(normed, grad_upward)
    upbias_part = jnp.sum(grad_upward.astype(jnp.float32), axis=0)
    grad_heads = grad_attended.reshape(query_blocks, query_block, heads_local, HD)
    deltas = jnp.transpose(
        jnp.sum(grad_heads.astype(jnp.float32) * attn_blocks, axis=-1), (0, 2, 1)
    )
    query_stack = (
        query_heads,
        grad_heads,
        log_totals,
        deltas,
        qrow_blocks,
        qpos_blocks,
        qpiece_blocks,
    )
    zero_block = jnp.zeros((key_block, heads_local, HD), jnp.float32)

    def key_step(grad_queries, key_args):
        key_vals, value_vals, key_row, key_pos, key_piece = key_args

        def query_step(kv_grads, query_args):
            (
                query_vals,
                grad_vals,
                log_total,
                delta_row,
                query_row,
                query_pos,
                query_piece,
            ), grad_query = query_args
            visible_pairs = visible(query_row, query_pos, query_piece, key_row, key_pos, key_piece)

            def query_update(states):
                grad_key, grad_value, grad_query = states
                softmax_low, grad_scores = pair_grads(
                    query_vals,
                    grad_vals,
                    log_total,
                    delta_row,
                    key_vals,
                    value_vals,
                    visible_pairs,
                    score_scale,
                )
                grad_value = grad_value + jnp.einsum(
                    "hqk,qhd->khd", softmax_low, grad_vals, preferred_element_type=jnp.float32
                )
                grad_query = (
                    grad_query
                    + jnp.einsum(
                        "hqk,khd->qhd", grad_scores, key_vals, preferred_element_type=jnp.float32
                    )
                    * score_scale
                )
                grad_key = (
                    grad_key
                    + jnp.einsum(
                        "hqk,qhd->khd", grad_scores, query_vals, preferred_element_type=jnp.float32
                    )
                    * score_scale
                )
                return (grad_key, grad_value, grad_query)

            grad_key, grad_value, grad_query = lax.cond(
                jnp.any(visible_pairs),
                query_update,
                unchanged,
                (kv_grads[0], kv_grads[1], grad_query),
            )
            return ((grad_key, grad_value), grad_query)

        (grad_key, grad_value), grad_queries = lax.scan(
            query_step, (zero_block, zero_block), (query_stack, grad_queries)
        )
        return (grad_queries, (grad_key, grad_value))

    grad_queries, (grad_keys, grad_values) = lax.scan(
        key_step, jnp.zeros(query_heads.shape, jnp.float32), key_stack
    )
    key_grad_local, value_grad_local = (
        lax.psum_scatter(
            grad_keys.reshape(whole_rows, width_local).astype(jnp.bfloat16),
            "ctx",
            scatter_dimension=0,
            tiled=True,
        ).astype(jnp.float32),
        lax.psum_scatter(
            grad_values.reshape(whole_rows, width_local).astype(jnp.bfloat16),
            "ctx",
            scatter_dimension=0,
            tiled=True,
        ).astype(jnp.float32),
    )
    _, turn_back = jax.vjp(lambda values: rotate(values, angles), packed[0])
    grad_packed = jnp.stack(
        [
            turn_back(grad_queries.reshape(length, width_local))[0],
            turn_back(key_grad_local)[0],
            value_grad_local,
        ]
    ).astype(jnp.bfloat16)
    inproj_full = jnp.einsum("td,jte->jde", normed, grad_packed, preferred_element_type=jnp.float32)
    inbias_part = jnp.sum(grad_packed.astype(jnp.float32), axis=1)
    inproj_grad, outproj_grad, upproj_grad, downproj_grad = (
        lax.psum_scatter(
            inproj_full.astype(jnp.bfloat16), ("fsdp", "ctx"), scatter_dimension=1, tiled=True
        ).astype(jnp.float32),
        lax.psum_scatter(
            outproj_full.astype(jnp.bfloat16), ("fsdp", "ctx"), scatter_dimension=1, tiled=True
        ).astype(jnp.float32),
        lax.psum_scatter(
            upproj_full.astype(jnp.bfloat16), ("fsdp", "ctx"), scatter_dimension=0, tiled=True
        ).astype(jnp.float32),
        lax.psum_scatter(
            downproj_full.astype(jnp.bfloat16), ("fsdp", "ctx"), scatter_dimension=1, tiled=True
        ).astype(jnp.float32),
    )
    grad_normed = lax.psum_scatter(
        (
            jnp.einsum("jte,jde->td", grad_packed, inproj_back, preferred_element_type=jnp.float32)
            + dot_last(grad_upward, upproj_back)
        ).astype(jnp.bfloat16),
        "tp",
        scatter_dimension=0,
        tiled=True,
    ).astype(jnp.float32)
    _, norm_back = jax.vjp(layer_norm, token_share, gain_full, shift_full)
    grad_tokens, gain_part, shift_part = norm_back(grad_normed)
    cot_share = lax.dynamic_slice_in_dim(cotangent, share_start, share_rows, 0).astype(jnp.float32)
    input_grad = (cot_share + grad_tokens).astype(jnp.bfloat16)
    outbias_part = jnp.sum(cot_share, axis=0)
    gain_grad, shift_grad, outbias_grad = lax.psum(
        (gain_part, shift_part, outbias_part), ("fsdp", "ctx", "tp")
    )
    inbias_grad, upbias_grad = lax.psum((inbias_part, upbias_part), ("fsdp", "ctx"))
    return (
        layer_out,
        input_grad,
        gain_grad,
        shift_grad,
        inproj_grad,
        inbias_grad,
        outproj_grad,
        upproj_grad,
        upbias_grad,
        downproj_grad,
        outbias_grad,
    )


def solution(mesh):
    return jax.shard_map(
        body,
        mesh=mesh,
        in_specs=(
            P(("fsdp", "ctx"), None),
            P(("fsdp", "ctx"), None),
            P(("fsdp", "ctx")),
            P(("fsdp", "ctx")),
            P(),
            P(),
            P(None, ("fsdp", "ctx"), "tp"),
            P(None, "tp"),
            P("tp", ("fsdp", "ctx")),
            P(("fsdp", "ctx"), "tp"),
            P("tp"),
            P("tp", ("fsdp", "ctx")),
            P(),
        ),
        out_specs=(
            P(("fsdp", "ctx", "tp"), None),
            P(("fsdp", "ctx", "tp"), None),
            P(),
            P(),
            P(None, ("fsdp", "ctx"), "tp"),
            P(None, "tp"),
            P("tp", ("fsdp", "ctx")),
            P(("fsdp", "ctx"), "tp"),
            P("tp"),
            P("tp", ("fsdp", "ctx")),
            P(),
        ),
        check_vma=False,
    )
```

profile of v0, /device:TPU:0, one launch (start us, length us, event | category | flops | bytes accessed | tf_op | source)
XLA Modules:
  0.0 1284.1 jit_solution(6912950896664452562)
XLA Ops:
  15.5 44.3 %all-gather.8.cloned.1.call-done = bf16[3,2048,512]{1,2,0:T(8,128)(2,1)} async-done(((bf16[3,256,512]{1,2,0:T(8,128)(2,1)}), bf16[3,2048,512]{1,2,0:T(8,128)(2,1)}) %all-gather.8.cloned.1.call-update) | async-done | bytes 6291472 | tf_op jit(solution)/shard_map/all_gather | solution.py:126
  98.1 28.6 %all-gather.10.cloned.1.call-done = bf16[4096,512]{0,1:T(8,128)(2,1)} async-done(((bf16[1024,512]{0,1:T(8,128)(2,1)}), bf16[4096,512]{0,1:T(8,128)(2,1)}) %all-gather.10.cloned.1.call-update) | async-done | bytes 4194320 | tf_op jit(solution)/shard_map/all_gather | solution.py:144
  140.5 22.7 %all-gather.18.cloned.1.call-done = bf16[1,4096,512]{1,2,0:T(8,128)(2,1)} async-done(((bf16[1,1024,512]{1,2,0:T(8,128)(2,1)}), bf16[1,4096,512]{1,2,0:T(8,128)(2,1)}) %all-gather.18.cloned.1.call-update) | async-done | bytes 4194320 | tf_op jit(solution)/shard_map/all_gather | solution.py:145
  178.6 72.5 %while.101 = (s32[]{:T(128)}, f32[2,512,8,64]{1,3,2,0:T(8,128)}, f32[2,8,512]{2,1,0:T(8,128)S(1)}, s32[2,512]{1,0:T(2,128)S(1)}, s32[2,512]{1,0:T(2,128)S(1)}, /...) while((s32[]{:T(128)}, f32[2,512,8,64]{1,3,2,0:T(8,128)}, ...), condition=%wide.region_10.11_spmd.clone, body=%wide.region_2.10_spmd.clone.sunk | while | flops 1124383744 | bytes 128903272 | solution.py:196
  179.4 34.4 %while.104 = (s32[]{:T(128)}, f32[8,512]{1,0:T(8,128)S(1)}, f32[8,512]{1,0:T(8,128)S(1)}, f32[512,8,64]{0,2,1:T(8,128)S(1)}, s32[512,1]{0,1:T(1,128)S(1)}, /*ind...) while((s32[]{:T(128)}, f32[8,512]{1,0:T(8,128)S(1)}, ...), condition=%wide.region_9.9_spmd, body=%wide.region_3.8_spmd.sunk | while | flops 1124108288 | bytes 124575024 | solution.py:192
  181.8 24.7 %conditional.6 = ((f32[8,512]{1,0:T(8,128)S(1)}, f32[8,512]{1,0:T(8,128)S(1)}, f32[512,8,64]{0,2,1:T(8,128)S(1)})) conditional(s32[]{:T(128)} %convert_element_type.261, (f32[8,512]{1,0:T(8,128)S(1)}, f32[8,512]{1,0:T(8,128)S(1)}, f32[512,8,64]{0,2,1:T(8,128)S(1)}) %tuple.223, (pred[512,1024]{0,1:T(8,128)(4,1)S(1)}, ...), branch_computations={%region_5.4_spmd, %region_6.7_spmd} | conditional | flops 1120415744 | bytes 123995192 | solution.py:185
  215.2 34.7 %while.104 = (s32[]{:T(128)}, f32[8,512]{1,0:T(8,128)S(1)}, f32[8,512]{1,0:T(8,128)S(1)}, f32[512,8,64]{0,2,1:T(8,128)S(1)}, s32[512,1]{0,1:T(1,128)S(1)}, /*ind...) while((s32[]{:T(128)}, f32[8,512]{1,0:T(8,128)S(1)}, ...), condition=%wide.region_9.9_spmd, body=%wide.region_3.8_spmd.sunk | while | flops 1124108288 | bytes 124575024 | solution.py:192
  217.7 24.9 %conditional.6 = ((f32[8,512]{1,0:T(8,128)S(1)}, f32[8,512]{1,0:T(8,128)S(1)}, f32[512,8,64]{0,2,1:T(8,128)S(1)})) conditional(s32[]{:T(128)} %convert_element_type.261, (f32[8,512]{1,0:T(8,128)S(1)}, f32[8,512]{1,0:T(8,128)S(1)}, f32[512,8,64]{0,2,1:T(8,128)S(1)}) %tuple.223, (pred[512,1024]{0,1:T(8,128)(4,1)S(1)}, ...), branch_computations={%region_5.4_spmd, %region_6.7_spmd} | conditional | flops 1120415744 | bytes 123995192 | solution.py:185
  257.1 156.7 %while.103 = (s32[]{:T(128)}, f32[2,512,8,64]{1,3,2,0:T(8,128)}, bf16[4,1024,8,64]{1,3,2,0:T(8,128)(2,1)}, bf16[4,1024,8,64]{1,3,2,0:T(8,128)(2,1)}, s32[4,1024]...) while((s32[]{:T(128)}, f32[2,512,8,64]{1,3,2,0:T(8,128)}, ...), condition=%wide.region_19.20_spmd.clone, body=%wide.region_13.19_spmd.clone.sunk | while | flops 2732091392 | bytes 158286896 | solution.py:303
  264.9 75.9 %while.105 = (s32[]{:T(128)}, f32[1024,8,64]{0,2,1:T(8,128)}, f32[1024,8,64]{0,2,1:T(8,128)}, f32[2,512,8,64]{1,3,2,0:T(8,128)}, s32[2,512]{1,0:T(2,128)S(1)}, /...) while((s32[]{:T(128)}, f32[1024,8,64]{0,2,1:T(8,128)}, ...), condition=%wide.region_18.18_spmd.clone, body=%wide.region_14.17_spmd.clone.sunk | while | flops 2732086272 | bytes 141205552 | solution.py:298
  269.5 32.4 %conditional.5 = (f32[1024,8,64]{0,2,1:T(8,128)}, f32[1024,8,64]{0,2,1:T(8,128)}, f32[1,512,8,64]{1,3,2,0:T(8,128)S(1)}) conditional(s32[]{:T(128)} %convert_element_type.260, (f32[1024,8,64]{0,2,1:T(8,128)}, f32[1024,8,64]{0,2,1:T(8,128)}, f32[512,8,64]{0,2,1:T(8,128)S(1)}) %tuple.241, (pred[512,1024]{1,0:T(8,128)(4,1)}, ...), branch_computations={%region_16.15_spmd, %region_17.16_spmd} | conditional | flops 2728394752 | bytes 136429824 | solution.py:290
  307.6 32.1 %conditional.5 = (f32[1024,8,64]{0,2,1:T(8,128)}, f32[1024,8,64]{0,2,1:T(8,128)}, f32[1,512,8,64]{1,3,2,0:T(8,128)S(1)}) conditional(s32[]{:T(128)} %convert_element_type.260, (f32[1024,8,64]{0,2,1:T(8,128)}, f32[1024,8,64]{0,2,1:T(8,128)}, f32[512,8,64]{0,2,1:T(8,128)S(1)}) %tuple.241, (pred[512,1024]{1,0:T(8,128)(4,1)}, ...), branch_computations={%region_16.15_spmd, %region_17.16_spmd} | conditional | flops 2728394752 | bytes 136429824 | solution.py:290
  352.3 11.4 while.105
  375.3 11.4 while.105
  398.1 11.4 while.105
  433.8 11.8 reshape.443
  446.4 14.7 %fusion.76 = f32[1024,2048]{1,0:T(8,128)} fusion(bf16[2048,2048]{1,0:T(8,128)(2,1)} %all-gather.14.cloned.1.call-done, bf16[1024,2048]{1,0:T(8,128)(2,1)} %param.25, f32[2048]{0:T(1024)S(1)} %copy-done.36, f32[2048]{0:T(1024)S(1)} %copy-done.30, f32[1024]{0:T(1024)S(1)} %copy-done.43, f32[1024]{0:T(1024)S(1)} %copy-done.34), kind=kOutput, calls=%fused_computation.176 | convolution fusion | flops 8602517504 | bytes 20996096 | tf_op jit(solution)/shard_map/dot_general | solution.py:200
  467.1 18.9 %convert_reduce_fusion = (f32[2048]{0:T(1024)S(1)}, bf16[1024,2048]{1,0:T(8,128)(2,1)S(1)}) fusion(f32[1024,2048]{1,0:T(8,128)} %fusion.76, f32[2048]{0:T(1024)S(1)} %convert_element_type.162, bf16[1024,2048]{1,0:T(8,128)(2,1)} %param.26, bf16[2048,2048]{1,0:T(8,128)(2,1)} %all-gather.16.cloned.1.call-done), kind=kOutput, calls=%fused_computation.113 | convolution fusion | flops 8638167040 | bytes 25182208 | tf_op jit(solution)/shard_map/dot_general | solution.py:52
  488.0 12.3 convolution_convert_fusion.1
  500.4 16.0 %convolution_convert_fusion = bf16[2048,2048]{1,0:T(8,128)(2,1)} fusion(bf16[1024,2048]{1,0:T(8,128)(2,1)} %param.26, f32[1024,2048]{1,0:T(8,128)} %fusion.76, f32[2048]{0:T(1024)S(1)} %convert_element_type.162), kind=kOutput, calls=%fused_computation.118 | convolution fusion | flops 8615100416 | bytes 20979712 | tf_op jit(solution)/shard_map/dot_general | solution.py:61
  516.6 14.7 %fusion.83 = f32[1024,2048]{1,0:T(8,128)} fusion(bf16[1024,2048]{1,0:T(8,128)(2,1)} %copy-done.45, bf16[2048,2048]{1,0:T(8,128)(2,1)} %all-gather.14.cloned.1.call-done), kind=kOutput, calls=%fused_computation.182 | convolution fusion | flops 8589934592 | bytes 20971520 | tf_op jit(solution)/shard_map/dot_general | solution.py:52
  532.8 274.5 %reduce-scatter.11.cloned.1.call-done = bf16[1024,512]{0,1:T(8,128)(2,1)} async-done(((bf16[4096,512]{0,1:T(8,128)(2,1)}), bf16[1024,512]{0,1:T(8,128)(2,1)}) %reduce-scatter.11.cloned.1.call-update) | async-done | bytes 1048592 | tf_op jit(solution)/shard_map/reduce_scatter | solution.py:307
  815.3 39.3 %reduce-scatter.13.cloned.1.call-done = bf16[1024,512]{1,0:T(8,128)(2,1)} async-done(((bf16[4096,512]{1,0:T(8,128)(2,1)}), bf16[1024,512]{1,0:T(8,128)(2,1)}) %reduce-scatter.13.cloned.1.call-update) | async-done | bytes 1048592 | tf_op jit(solution)/shard_map/reduce_scatter | solution.py:313
  854.6 12.4 fusion.62
  867.1 16.6 %fusion.75 = f32[1024,2048]{1,0:T(8,128)S(1)} fusion(bf16[2048,2048]{1,0:T(8,128)(2,1)} %all-gather.16.cloned.1.call-done, f32[1024,2048]{1,0:T(8,128)} %fusion.76, f32[2048]{0:T(1024)S(1)} %convert_element_type.162), kind=kOutput, calls=%fused_computation.175 | convolution fusion | flops 8610906112 | bytes 25174016 | tf_op jit(solution)/shard_map/dot_general | solution.py:207
  889.4 11.8 convert_bitcast_fusion
  914.8 51.5 %all-reduce.7 = (f32[3,512]{1,0:T(4,128)}, f32[2048]{0:T(1024)}) all-reduce(f32[3,512]{1,0:T(4,128)S(1)} %convert_reduce_fusion.1, f32[2048]{0:T(1024)S(1)} %get-tuple-element.1491), channel_id=1, replica_groups=mesh['fsdp'=2,'ctx'=4,'tp'=4] {'fsdp','ctx'}, use_global_device_ids=true, to_apply=%region_33.34 | all-reduce | flops 3584 | bytes 28672 | tf_op jit(solution)/shard_map/psum | solution.py:361
  977.7 72.0 %reduce-scatter.23.cloned.1.call-done = bf16[2048,256]{1,0:T(8,128)(2,1)} async-done(((bf16[2048,2048]{1,0:T(8,128)(2,1)}), bf16[2048,256]{1,0:T(8,128)(2,1)}) %reduce-scatter.23.cloned.1.call-update) | async-done | bytes 1048592 | tf_op jit(solution)/shard_map/reduce_scatter | solution.py:340
  1052.4 76.3 %reduce-scatter.15.cloned.1.call-done = bf16[256,2048]{1,0:T(8,128)(2,1)} async-done(((bf16[1024,2048]{1,0:T(8,128)(2,1)}), bf16[256,2048]{1,0:T(8,128)(2,1)}) %reduce-scatter.15.cloned.1.call-update) | async-done | bytes 1048592 | tf_op jit(solution)/shard_map/reduce_scatter | solution.py:344
  1131.4 76.9 %reduce-scatter.9.cloned.1.call-done = bf16[256,2048]{1,0:T(8,128)(2,1)} async-done(((bf16[1024,2048]{1,0:T(8,128)(2,1)}), bf16[256,2048]{1,0:T(8,128)(2,1)}) %reduce-scatter.9.cloned.1.call-update) | async-done | bytes 1048592 | tf_op jit(solution)/shard_map/reduce_scatter | solution.py:204
  1214.9 41.6 %all-reduce.6 = (f32[2048]{0:T(1024)}, f32[2048]{0:T(1024)}, f32[2048]{0:T(1024)}) all-reduce(f32[2048]{0:T(1024)S(1)} %get-tuple-element.1353, f32[2048]{0:T(1024)S(1)} %get-tuple-element.1355, f32[2048]{0:T(1024)S(1)} %get-tuple-element.1509), channel_id=1, replica_groups=mesh['fsdp'=2,'ctx'=4,'tp'=4] {'fsdp','ctx','tp'}, use_global_device_ids=true, to_apply=%region_28.29 | all-reduce | flops 6144 | bytes 49152 | tf_op jit(solution)/shard_map/psum | solution.py:358
  1256.5 18.3 %reduce-scatter.17.cloned.1.call-done = bf16[3,256,512]{1,2,0:T(8,128)(2,1)} async-done(((bf16[3,2048,512]{1,2,0:T(8,128)(2,1)}), bf16[3,256,512]{1,2,0:T(8,128)(2,1)}) %reduce-scatter.17.cloned.1.call-update) | async-done | bytes 786448 | tf_op jit(solution)/shard_map/reduce_scatter | solution.py:331
  (457 shorter events, 380.7 us)
Async XLA Ops:
  7.2 52.7 %all-gather.8.cloned.1.call-start = ((), (), s32[]{:S(2)}) async-start(), calls=%async_computation.8 | async-start | bytes 7077888 | tf_op jit(solution)/shard_map/all_gather | solution.py:126
  9.5 80.5 %all-gather.12.cloned.1.call-start = ((), (), s32[]{:S(2)}) async-start(), calls=%async_computation.10 | async-start | bytes 2359296 | tf_op jit(solution)/shard_map/all_gather | solution.py:127
  10.3 116.3 %all-gather.10.cloned.1.call-start = ((), (), s32[]{:S(2)}) async-start(), calls=%async_computation.9 | async-start | bytes 5242880 | tf_op jit(solution)/shard_map/all_gather | solution.py:144
  13.8 56.5 %copy-start.33 = (f32[1024]{0:T(1024)}, f32[1024]{0:T(1024)S(1)}, u32[]{:S(2)}) copy-start(f32[1024]{0:T(1024)S(1)} %broadcast_multiply_fusion) | copy-start | bytes 12292
  15.1 55.3 %copy-start.29 = (f32[2048]{0:T(1024)}, f32[2048]{0:T(1024)S(1)}, u32[]{:S(2)}) copy-start(f32[2048]{0:T(1024)S(1)} %convert_element_type.152) | copy-start | bytes 24580
  15.1 55.2 %copy-start.35 = (f32[2048]{0:T(1024)}, f32[2048]{0:T(1024)S(1)}, u32[]{:S(2)}) copy-start(f32[2048]{0:T(1024)S(1)} %convert_element_type.153) | copy-start | bytes 24580
  15.2 55.2 %copy-start.42 = (f32[1024]{0:T(1024)}, f32[1024]{0:T(1024)S(1)}, u32[]{:S(2)}) copy-start(f32[1024]{0:T(1024)S(1)} %add_rsqrt_fusion) | copy-start | bytes 12292
  15.5 57.6 %copy-start.24 = (f32[1024,16]{0,1:T(8,128)}, f32[1024,16]{0,1:T(8,128)S(1)}, u32[]{:S(2)}) copy-start(f32[1024,16]{0,1:T(8,128)S(1)} %get-tuple-element.1523) | copy-start | bytes 196612
  15.5 57.6 %copy-start.26 = (f32[1024,16]{0,1:T(8,128)}, f32[1024,16]{0,1:T(8,128)S(1)}, u32[]{:S(2)}) copy-start(f32[1024,16]{0,1:T(8,128)S(1)} %get-tuple-element.1524) | copy-start | bytes 196612
  74.7 9.2 copy-start.32
  74.7 88.4 %all-gather.18.cloned.1.call-start = ((), (), s32[]{:S(2)}) async-start(), calls=%async_computation.21 | async-start | bytes 5242880 | tf_op jit(solution)/shard_map/all_gather | solution.py:145
  77.5 368.8 %all-gather.14.cloned.1.call-start = ((), (), s32[]{:S(2)}) async-start(), calls=%async_computation.11 | async-start | bytes 9437184 | tf_op jit(solution)/shard_map/all_gather | solution.py:128
  78.1 388.9 %all-gather.16.cloned.1.call-start = ((), (), s32[]{:S(2)}) async-start(), calls=%async_computation.12 | async-start | bytes 9437184 | tf_op jit(solution)/shard_map/all_gather | solution.py:129
  78.7 728.7 %reduce-scatter.11.cloned.1.call-start = ((), (), s32[]{:S(2)}) async-start(), calls=%async_computation.14 | async-start | bytes 5242880 | tf_op jit(solution)/shard_map/reduce_scatter | solution.py:307
  269.5 8.5 copy-start.4
  278.0 9.7 copy-start.1
  315.8 9.7 copy-start.1
  423.7 430.9 %reduce-scatter.13.cloned.1.call-start = ((), (), s32[]{:S(2)}) async-start(), calls=%async_computation.15 | async-start | bytes 5242880 | tf_op jit(solution)/shard_map/reduce_scatter | solution.py:313
  445.7 466.8 %reduce-scatter.19.cloned.1.call-start = ((), (), s32[]{:S(2)}) async-start(), calls=%async_computation.18 | async-start | bytes 2359296 | tf_op jit(solution)/shard_map/reduce_scatter | solution.py:334
  446.3 14.8 %copy-start.10 = (f32[2,512,8,64]{1,3,2,0:T(8,128)S(1)}, f32[2,512,8,64]{1,3,2,0:T(8,128)}, u32[]{:S(2)}) copy-start(f32[2,512,8,64]{1,3,2,0:T(8,128)} %get-tuple-element.1124) | copy-start | bytes 6291460
  467.0 508.0 %reduce-scatter.21.cloned.1.call-start = ((), (), s32[]{:S(2)}) async-start(), calls=%async_computation.19 | async-start | bytes 9437184 | tf_op jit(solution)/shard_map/reduce_scatter | solution.py:337
  467.0 21.0 %copy-start.8 = (bf16[1024,2048]{1,0:T(8,128)(2,1)S(1)}, bf16[1024,2048]{1,0:T(8,128)(2,1)}, u32[]{:S(2)}) copy-start(bf16[1024,2048]{1,0:T(8,128)(2,1)} %param.25) | copy-start | bytes 12582916
  500.4 549.3 %reduce-scatter.23.cloned.1.call-start = ((), (), s32[]{:S(2)}) async-start(), calls=%async_computation.20 | async-start | bytes 9437184 | tf_op jit(solution)/shard_map/reduce_scatter | solution.py:340
  516.5 14.7 %copy-start.3 = (f32[2,512,8,64]{1,3,2,0:T(8,128)S(1)}, f32[2,512,8,64]{1,3,2,0:T(8,128)}, u32[]{:S(2)}) copy-start(f32[2,512,8,64]{1,3,2,0:T(8,128)} %get-tuple-element.1126) | copy-start | bytes 6291460
  516.5 612.2 %reduce-scatter.15.cloned.1.call-start = ((), (), s32[]{:S(2)}) async-start(), calls=%async_computation.16 | async-start | bytes 5242880 | tf_op jit(solution)/shard_map/reduce_scatter | solution.py:344
  531.4 279.5 %copy-start.25 = (f32[1024,16]{0,1:T(8,128)S(1)}, f32[1024,16]{0,1:T(8,128)}, u32[]{:S(2)}) copy-start(f32[1024,16]{0,1:T(8,128)} %copy-done.24) | copy-start | bytes 196612
  531.4 279.5 %copy-start.27 = (f32[1024,16]{0,1:T(8,128)S(1)}, f32[1024,16]{0,1:T(8,128)}, u32[]{:S(2)}) copy-start(f32[1024,16]{0,1:T(8,128)} %copy-done.26) | copy-start | bytes 196612
  532.8 278.1 %copy-start.13 = (f32[2,8,8,8,512]{4,3,0,2,1:T(8,128)S(1)}, f32[2,8,8,8,512]{4,3,0,2,1:T(8,128)}, u32[]{:S(2)}) copy-start(f32[2,8,8,8,512]{4,3,0,2,1:T(8,128)} %copy-done.12) | copy-start | bytes 6291460
  867.1 16.7 %copy-start.23 = (bf16[64,8,2,512]{3,1,2,0:T(8,128)(2,1)S(1)}, bf16[64,8,2,512]{3,1,2,0:T(8,128)(2,1)}, u32[]{:S(2)}) copy-start(bf16[64,8,2,512]{3,1,2,0:T(8,128)(2,1)} %copy-done.22) | copy-start | bytes 3145732
  867.1 341.2 %reduce-scatter.9.cloned.1.call-start = ((), (), s32[]{:S(2)}) async-start(), calls=%async_computation.13 | async-start | bytes 5242880 | tf_op jit(solution)/shard_map/reduce_scatter | solution.py:204
  867.1 16.7 %copy-start.44 = (bf16[512,2048]{1,0:T(8,128)(2,1)S(1)}, bf16[512,2048]{1,0:T(8,128)(2,1)}, u32[]{:S(2)}) copy-start(bf16[512,2048]{1,0:T(8,128)(2,1)} %all-gather.12.cloned.1.call-done) | copy-start | bytes 6291460
  888.2 386.7 %reduce-scatter.17.cloned.1.call-start = ((), (), s32[]{:S(2)}) async-start(), calls=%async_computation.17 | async-start | bytes 7077888 | tf_op jit(solution)/shard_map/reduce_scatter | solution.py:331
  (48 other events, 207.9 us)
Sparse Core Ops, SparseCore 0:
  10.5 49.3 all-gather.7
  61.7 28.1 all-gather.11
  92.1 34.4 all-gather.9
  128.6 34.4 all-gather.17
  164.9 54.3 all-gather.13
  221.0 55.9 all-gather.15
  423.8 383.4 reduce-scatter.10
  810.0 44.5 reduce-scatter.12
  858.5 41.2 reduce-scatter.18
  903.4 71.5 reduce-scatter.20
  978.4 71.2 reduce-scatter.22
  1052.0 76.7 reduce-scatter.14
  1131.0 77.2 reduce-scatter.8
  1211.9 62.8 reduce-scatter.16
where the time goes:
time: 1290 us; the launch traced here: 1280 us
  waiting for transfers between devices  664 us (51%)
  matrix products  222 us (17%)
  local copies, waits for them, and re-layouts  165 us (13%)
  blocking collectives  104 us (8%)
  other arithmetic  101 us (8%)
  between operations  14.7 us (1%)
  loops' own time  13.6 us (1%)
    reduce_scatter x1, waiting for transfers between devices, body(): lax.psum_scatter(grad_keys.reshape(whole_rows, width_local).astype(jnp.bf...  275 us
    reduce_scatter x1, waiting for transfers between devices, body(): lax.psum_scatter((jnp.dot(attended, outproj_all, preferred_element_type=j...  76.9 us
    reduce_scatter x1, waiting for transfers between devices, body(): lax.psum_scatter((jnp.einsum('jte,jde->td', grad_packed, inproj_back, pre...  76.3 us
    reduce_scatter x1, waiting for transfers between devices, body(): lax.psum_scatter(downproj_full.astype(jnp.bfloat16), ('fsdp', 'ctx'), sca...  72 us
    psum x1, blocking collectives, body(): lax.psum((inbias_part, upbias_part), ('fsdp', 'ctx'))  51.5 us
    all_gather x1, waiting for transfers between devices, body(): lax.all_gather(in_proj, ('fsdp', 'ctx'), axis=1, tiled=True)  44.3 us
    psum x1, blocking collectives, body(): lax.psum((gain_part, shift_part, outbias_part), ('fsdp', 'ctx', 'tp'))  41.6 us
    reduce_scatter x1, waiting for transfers between devices, body(): lax.psum_scatter(grad_values.reshape(whole_rows, width_local).astype(jnp....  39.3 us
  transfers between devices with their start and end apart: 14, of which 10 were waited for; matrix products, arithmetic and copies ran while one was open for 36% of the time, Pallas kernels for 0%

commit v1 on v0

v1 whole, which is shorter than its diff:
```python
import functools
import math

import jax
import jax.numpy as jnp
from jax import lax
from jax.experimental import pallas as pl
from jax.experimental.pallas import tpu as pltpu
from jax.sharding import Mesh
from jax.sharding import PartitionSpec as P

HD = 64
ROT = 32
RUN = 256
EPS = 1e-05
NEG = -1e30
F32 = jnp.float32
BF = jnp.bfloat16
NN = (((1,), (0,)), ((), ()))
NT = (((1,), (1,)), ((), ()))
TN = (((0,), (0,)), ((), ()))
SWAP = [(0, 1), (1, 0)]
GELU_A = math.sqrt(2.0 / math.pi)
GELU_B = 0.044715


def dot(a, b, dims=NN):
    return lax.dot_general(a, b, dims, preferred_element_type=F32)


def call(body, name, grid, in_specs, out_specs, out_shape, scratch, flops, moved, prefetch=1, vmem=56):
    return pl.pallas_call(
        body,
        out_shape=out_shape,
        grid_spec=pltpu.PrefetchScalarGridSpec(
            num_scalar_prefetch=prefetch,
            grid=grid,
            in_specs=in_specs,
            out_specs=out_specs,
            scratch_shapes=scratch,
        ),
        compiler_params=pltpu.CompilerParams(
            vmem_limit_bytes=vmem << 20, dimension_semantics=("arbitrary",) * len(grid)
        ),
        cost_estimate=pl.CostEstimate(flops=int(flops), bytes_accessed=int(moved), transcendentals=0),
        name=name,
    )


def row_block(size, width):
    return pl.BlockSpec((size, width), lambda i, s: (i, 0))


def fixed(shape, index=None):
    place = index or (0,) * len(shape)
    return pl.BlockSpec(shape, lambda i, s: place, pipeline_mode=pl.Buffered(1))


def norm_parts(rows):
    center = rows - jnp.mean(rows, axis=-1, keepdims=True)
    inverse = lax.rsqrt(jnp.mean(center * center, axis=-1, keepdims=True) + EPS)
    return center * inverse, inverse


def lanes_of(info, chunk, piece):
    return pl.ds(pl.multiple_of((piece ^ info[0]) * chunk, chunk), chunk)


def prepare_body(info, tok, cot, gain, shift, nrm, cot_out, cot_sum, *, chunk):
    xhat, _ = norm_parts(tok[...].astype(F32))
    full = (xhat * gain[...].astype(F32) + shift[...].astype(F32)).astype(BF)
    pieces = tok.shape[1] // chunk

    @pl.when(pl.program_id(0) == 0)
    def _():
        cot_sum[...] = jnp.zeros_like(cot_sum)

    cot_sum[...] += jnp.sum(cot[...].astype(F32), axis=0, keepdims=True)
    for r in range(pieces):
        nrm[:, lanes_of(info, chunk, r)] = full[:, r * chunk : r * chunk + chunk]
        cot_out[:, lanes_of(info, chunk, r)] = cot[:, r * chunk : r * chunk + chunk]


def prepare(info, tok, cot, gain, shift, chunk):
    rows, width = tok.shape
    size = min(rows, 256)
    spec = row_block(size, width)
    return call(
        functools.partial(prepare_body, chunk=chunk),
        "normalize",
        (rows // size,),
        [spec, spec, fixed((1, width)), fixed((1, width))],
        [spec, spec, pl.BlockSpec((1, width), lambda i, s: (0, 0))],
        [jax.ShapeDtypeStruct(tok.shape, BF)] * 2 + [jax.ShapeDtypeStruct((1, width), F32)],
        [],
        10 * tok.size,
        8 * tok.size,
    )(info, tok, cot, gain[None], shift[None])


def turn(values, cos_part, down, up):
    return (
        values * cos_part
        + pltpu.roll(values, 128 - ROT // 2, 1) * down
        + pltpu.roll(values, ROT // 2, 1) * up
    )


def project_body(info, nrm, cot, weights, bias, cos_t, down_t, up_t, q_out, kv_out, do_out, *, width):
    packed = dot(nrm[...], weights[:, : 3 * width]) + bias[...].astype(F32)
    c, d, u = cos_t[...], down_t[...], up_t[...]
    for p in range(width // 128):
        lanes = slice(128 * p, 128 * p + 128)
        q_out[:, lanes] = turn(packed[:, lanes], c, d, u).astype(BF)
        shifted = slice(width + 128 * p, width + 128 * p + 128)
        kv_out[:, lanes] = turn(packed[:, shifted], c, d, u).astype(BF)
    kv_out[:, width:] = packed[:, 2 * width :].astype(BF)
    do_out[...] = dot(cot[...], weights[:, 3 * width :]).astype(BF)


def project(info, nrm, cot, weights, bias, tables, width):
    rows, depth = nrm.shape
    size = min(rows, 256)
    spec = row_block(size, depth)
    table = row_block(size, 128)
    return call(
        functools.partial(project_body, width=width),
        "project",
        (rows // size,),
        [spec, spec, fixed((depth, 4 * width)), fixed((1, 3 * width)), table, table, table],
        [row_block(size, width), row_block(size, 2 * width), row_block(size, width)],
        [
            jax.ShapeDtypeStruct((rows, width), BF),
            jax.ShapeDtypeStruct((rows, 2 * width), BF),
            jax.ShapeDtypeStruct((rows, width), BF),
        ],
        [],
        2 * rows * depth * 4 * width,
        2 * (2 * rows * depth + depth * 4 * width + 4 * rows * width),
    )(info, nrm, cot, weights, bias, *tables)


def hidden_body(info, nrm, cot, up, down, bias, act_out, grad_out, sum_out):
    u = dot(nrm[...], up[...]) + bias[...].astype(F32)
    g = dot(cot[...], down[...])
    square = u * u
    t = jnp.tanh(GELU_A * (u + GELU_B * square * u))
    half = 0.5 * (1.0 + t)
    act_out[...] = (u * half).astype(BF)
    slope = half + 0.5 * u * (1.0 - t * t) * (GELU_A * (1.0 + 3.0 * GELU_B * square))
    low = (g * slope).astype(BF)
    grad_out[...] = low

    @pl.when(pl.program_id(0) == 0)
    def _():
        sum_out[...] = jnp.zeros_like(sum_out)

    sum_out[...] += jnp.sum(low.astype(F32), axis=0, keepdims=True)


def hidden(info, nrm, cot, weights, bias, width):
    rows, depth = nrm.shape
    size = min(rows, 256)
    spec = row_block(size, depth)
    return call(
        hidden_body,
        "hidden",
        (rows // size,),
        [spec, spec, fixed((depth, width)), fixed((depth, width), (0, 1)), fixed((1, width))],
        [row_block(size, width), row_block(size, width), pl.BlockSpec((1, width), lambda i, s: (0, 0))],
        [jax.ShapeDtypeStruct((rows, width), BF)] * 2 + [jax.ShapeDtypeStruct((1, width), F32)],
        [],
        4 * rows * depth * width,
        2 * (2 * rows * depth + 2 * depth * width + 2 * rows * width),
    )(info, nrm, cot, weights, weights, bias)


def spread_body(info, a, b, wa, wb, *rest):
    total = dot(a[...], wa[...], NT) + dot(b[...], wb[...], NT)
    if len(rest) == 2:
        total = total + rest[0][...].astype(F32)
    rest[-1][...] = total.astype(BF)


def spread(info, a, b, wa, wb, ia, ib, half, rows, received, name):
    depth = wa.shape[0]
    size = min(rows, 256)
    first = half * (rows // size)
    at = lambda width: pl.BlockSpec((size, width), lambda i, s: (i + first, 0))
    wide_a, wide_b = a.shape[1], b.shape[1]
    extra = [] if received is None else [received]
    return call(
        spread_body,
        name,
        (rows // size,),
        [at(wide_a), at(wide_b), fixed((depth, wide_a), (0, ia)), fixed((depth, wide_b), (0, ib))]
        + [row_block(size, depth)] * len(extra),
        [row_block(size, depth)],
        [jax.ShapeDtypeStruct((rows, depth), BF)],
        [],
        2 * rows * depth * (wide_a + wide_b),
        2 * (rows + depth) * (wide_a + wide_b) + 2 * rows * depth * (1 + len(extra)),
    )(info, a, b, wa, wb, *extra)[0]


def outer_body(info, left, right, out):
    out[...] = dot(left[...], right[...], TN).astype(BF)


def outer(info, left, right, blocks, chunk, name):
    rows = left.shape[0]
    width = right.shape[1]
    size = min(chunk, 256)
    per = chunk // size
    first, step = blocks
    count = (left.shape[1] // chunk if step == 0 else 2) * per

    def place(i, s):
        return (0, i) if step == 0 else (0, (first + step * (i // per)) * per + i % per)

    return call(
        outer_body,
        name,
        (count,),
        [pl.BlockSpec((rows, size), place), fixed((rows, width))],
        [row_block(size, width)],
        [jax.ShapeDtypeStruct((count * size, width), BF)],
        [],
        2 * rows * count * size * width,
        2 * (rows * count * size + rows * width + count * size * width),
    )(info, left, right)[0]


def head_masks(block, scale):
    lane = lax.broadcasted_iota(jnp.int32, block.shape, 1)
    v = block.astype(F32) * scale
    return (jnp.where(lane < HD, v, 0.0).astype(BF), jnp.where(lane < HD, 0.0, v).astype(BF))


def own_mask(flag, width):
    kk = lax.broadcasted_iota(jnp.int32, (RUN, width), 0)
    qq = lax.broadcasted_iota(jnp.int32, (RUN, width), 1)
    return kk <= qq + flag * RUN


def each_prefix(here, half, runs, work):
    size = runs // 2
    while size:

        @pl.when((here & size) != 0)
        def _(size=size):
            low = here & ((runs - 1) & ~(2 * size - 1))
            work(pl.multiple_of((low ^ half) * RUN, RUN), size * RUN)

        size //= 2


def forward_body(info, q_ref, do_ref, k_ref, v_ref, kx_ref, vx_ref, att_ref, stat_ref, vt, vxt, acc, ml, *, pairs, cut):
    i = pl.program_id(0)
    half = info[0]
    here = i ^ half
    has_cross = info[1]
    heads = 2 * pairs
    runs = k_ref.shape[0] // RUN

    @pl.when(i == 0)
    def _():
        vt[...] = v_ref[...].astype(F32).T.astype(BF)

    @pl.when((i == 0) & (has_cross > 0))
    def _():
        vxt[...] = vx_ref[...].astype(F32).T.astype(BF)

    qm = [head_masks(q_ref[:, 128 * p : 128 * p + 128], 1.0 / math.sqrt(HD)) for p in range(pairs)]

    def block(k_r, vt_r, start, size, mask=None):
        def score(n):
            p, h = divmod(n, 2)
            s = dot(k_r[pl.ds(start, size), 128 * p : 128 * p + 128], qm[p][h], NT)
            return s if mask is None else jnp.where(mask, s, NEG)

        def rest(n, s):
            top = jnp.max(s, axis=0, keepdims=True)
            rows = slice(HD * n, HD * n + HD)
            vb = vt_r[rows, pl.ds(start, size)]
            if mask is not None:
                e = jnp.exp(s - top)
                ml[n : n + 1, :] = top
                ml[heads + n : heads + n + 1, :] = jnp.sum(e, axis=0, keepdims=True)
                acc[rows, :] = dot(vb, e.astype(BF))
            else:
                m = ml[n : n + 1, :]
                new = jnp.maximum(m, top)
                alpha = jnp.exp(m - new)
                e = jnp.exp(s - new)
                ml[n : n + 1, :] = new
                ml[heads + n : heads + n + 1, :] = (
                    ml[heads + n : heads + n + 1, :] * alpha + jnp.sum(e, axis=0, keepdims=True)
                )
                acc[rows, :] = acc[rows, :] * alpha + dot(vb, e.astype(BF))

        s = score(0)
        for n in range(heads):
            following = score(n + 1) if n + 1 < heads else None
            rest(n, s)
            s = following

    block(k_ref, vt, pl.multiple_of(i * RUN, RUN), RUN, own_mask(info[2 + i], q_ref.shape[0]))
    each_prefix(here, half, runs, lambda start, size: block(k_ref, vt, start, size))

    @pl.when(has_cross > 0)
    def _():
        def cross(j, c):
            block(kx_ref, vxt, pl.multiple_of(j * cut, cut), cut)
            return c

        lax.fori_loop(0, kx_ref.shape[0] // cut, cross, 0)

    for p in range(pairs):
        do_t = do_ref[:, 128 * p : 128 * p + 128].astype(F32).T
        parts = []
        for h in range(2):
            n = 2 * p + h
            m, l = ml[n : n + 1, :], ml[heads + n : heads + n + 1, :]
            o = acc[HD * n : HD * n + HD, :] / l
            parts.append(o)
            stat_ref[n : n + 1, :] = m + jnp.log(l)
            stat_ref[heads + n : heads + n + 1, :] = jnp.sum(o * do_t[HD * h : HD * h + HD, :], axis=0, keepdims=True)
        att_ref[:, 128 * p : 128 * p + 128] = jnp.concatenate(parts, axis=0).T.astype(BF)


def attend(info, q, do, kv, kvx):
    rows, width = q.shape
    pairs = width // 128
    cut = min(rows, 1024)
    blk = row_block(RUN, width)
    left, right = fixed((rows, width)), fixed((rows, width), (0, 1))
    return call(
        functools.partial(forward_body, pairs=pairs, cut=cut),
        "attend",
        (rows // RUN,),
        [blk, blk, left, right, left, right],
        [blk, pl.BlockSpec((4 * pairs, RUN), lambda i, s: (0, i))],
        [jax.ShapeDtypeStruct((rows, width), BF), jax.ShapeDtypeStruct((4 * pairs, rows), F32)],
        [
            pltpu.VMEM((width, rows), BF),
            pltpu.VMEM((width, rows), BF),
            pltpu.VMEM((width, RUN), F32),
            pltpu.VMEM((4 * pairs, RUN), F32),
        ],
        40e9,
        14 * rows * width,
    )(info, q, do, kv, kv, kvx, kvx)


def backward_body(info, q_ref, do_ref, stat_ref, k_ref, v_ref, kx_ref, vx_ref, dq_ref, dk_ref, dv_ref, dkvx_ref, kt, kxt, dqt, dkx, dvx, *, pairs, cut):
    i = pl.program_id(0)
    half = info[0]
    here = i ^ half
    has_cross = info[1]
    heads = 2 * pairs
    width = 128 * pairs
    scale = 1.0 / math.sqrt(HD)
    runs = k_ref.shape[0] // RUN

    @pl.when(i == 0)
    def _():
        kt[...] = k_ref[...].astype(F32).T.astype(BF)
        dk_ref[...] = jnp.zeros_like(dk_ref)
        dv_ref[...] = jnp.zeros_like(dv_ref)

    @pl.when((i == 0) & (has_cross > 0))
    def _():
        kxt[...] = kx_ref[...].astype(F32).T.astype(BF)
        dkx[...] = jnp.zeros_like(dkx)
        dvx[...] = jnp.zeros_like(dvx)

    qm = [head_masks(q_ref[:, 128 * p : 128 * p + 128], scale) for p in range(pairs)]
    dm = [head_masks(do_ref[:, 128 * p : 128 * p + 128], 1.0) for p in range(pairs)]
    dqt[...] = jnp.zeros_like(dqt)

    def block(k_r, v_r, kt_r, dk_r, dv_r, start, size, mask=None):
        def products(n):
            p, h = divmod(n, 2)
            lanes = slice(128 * p, 128 * p + 128)
            return (
                dot(k_r[pl.ds(start, size), lanes], qm[p][h], NT),
                dot(v_r[pl.ds(start, size), lanes], dm[p][h], NT),
            )

        def rest(n, s, g):
            p, h = divmod(n, 2)
            e = jnp.exp(s - stat_ref[n : n + 1, :])
            if mask is not None:
                e = jnp.where(mask, e, 0.0)
            ds = (e * (g - stat_ref[heads + n : heads + n + 1, :])).astype(BF)
            rows = slice(HD * n, HD * n + HD)
            dqt[rows, :] += dot(kt_r[rows, pl.ds(start, size)], ds)
            return dot(ds, qm[p][h]), dot(e.astype(BF), dm[p][h])

        now = products(0)
        before = None
        for n in range(heads):
            following = products(n + 1) if n + 1 < heads else None
            grads = rest(n, *now)
            now = following
            if n % 2:
                lanes = slice(HD * (n - 1), HD * (n + 1))
                dk_r[pl.ds(start, size), lanes] += before[0] + grads[0]
                dv_r[pl.ds(start, size), lanes] += before[1] + grads[1]
            before = grads

    @pl.when(has_cross > 0)
    def _():
        def cross(j, c):
            block(kx_ref, vx_ref, kxt, dkx, dvx, pl.multiple_of(j * cut, cut), cut)
            return c

        lax.fori_loop(0, kx_ref.shape[0] // cut, cross, 0)

    work = lambda start, size, mask=None: block(k_ref, v_ref, kt, dk_ref, dv_ref, start, size, mask)
    work(pl.multiple_of(i * RUN, RUN), RUN, own_mask(info[2 + i], q_ref.shape[0]))
    each_prefix(here, half, runs, work)
    dq_ref[...] = (dqt[...] * scale).T

    @pl.when(i == pl.num_programs(0) - 1)
    def _():
        @pl.when(has_cross > 0)
        def _():
            dkvx_ref[:, :width] = dkx[...].astype(BF)
            dkvx_ref[:, width:] = dvx[...].astype(BF)

        @pl.when(has_cross == 0)
        def _():
            dkvx_ref[...] = jnp.zeros_like(dkvx_ref)


def attend_back(info, q, do, stat, kv, kvx):
    rows, width = q.shape
    pairs = width // 128
    cut = min(rows, 1024)
    blk = row_block(RUN, width)
    left, right = fixed((rows, width)), fixed((rows, width), (0, 1))
    whole = pl.BlockSpec((rows, width), lambda i, s: (0, 0))
    acc = jax.ShapeDtypeStruct((rows, width), F32)
    return call(
        functools.partial(backward_body, pairs=pairs, cut=cut),
        "attend_back",
        (rows // RUN,),
        [blk, blk, pl.BlockSpec((4 * pairs, RUN), lambda i, s: (0, i)), left, right, left, right],
        [blk, whole, whole, pl.BlockSpec((rows, 2 * width), lambda i, s: (0, 0))],
        [acc, acc, acc, jax.ShapeDtypeStruct((rows, 2 * width), BF)],
        [
            pltpu.VMEM((width, rows), BF),
            pltpu.VMEM((width, rows), BF),
            pltpu.VMEM((width, RUN), F32),
            pltpu.VMEM((rows, width), F32),
            pltpu.VMEM((rows, width), F32),
        ],
        60e9,
        30 * rows * width,
    )(info, q, do, stat, kv, kv, kvx, kvx)


def collect_body(info, dq, dk, dv, other_k, other_v, cos_t, down_t, up_t, out, sums, *, width):
    c, d, u = cos_t[...], -down_t[...], -up_t[...]
    for p in range(width // 128):
        lanes = slice(128 * p, 128 * p + 128)
        out[:, lanes] = turn(dq[:, lanes], c, d, u).astype(BF)
        key = dk[:, lanes] + other_k[:, lanes].astype(F32)
        out[:, width + 128 * p : width + 128 * p + 128] = turn(key, c, d, u).astype(BF)
    out[:, 2 * width :] = (dv[...] + other_v[...].astype(F32)).astype(BF)

    @pl.when(pl.program_id(0) == 0)
    def _():
        sums[...] = jnp.zeros_like(sums)

    sums[...] += jnp.sum(out[...].astype(F32), axis=0, keepdims=True)


def collect(info, dq, dk, dv, other, tables):
    rows, width = dq.shape
    size = min(rows, 512)
    spec = row_block(size, width)
    table = row_block(size, 128)
    return call(
        functools.partial(collect_body, width=width),
        "collect",
        (rows // size,),
        [spec, spec, spec, spec, pl.BlockSpec((size, width), lambda i, s: (i, 1)), table, table, table],
        [row_block(size, 3 * width), pl.BlockSpec((1, 3 * width), lambda i, s: (0, 0))],
        [jax.ShapeDtypeStruct((rows, 3 * width), BF), jax.ShapeDtypeStruct((1, 3 * width), F32)],
        [],
        20 * rows * width,
        30 * rows * width,
    )(info, dq, dk, dv, other, other, *tables)


def input_body(info, grad, tok, cot, gain, out, *, chunk):
    xhat, inverse = norm_parts(tok[...].astype(F32))
    pieces = tok.shape[1] // chunk
    parts = [grad[:, lanes_of(info, chunk, r)] for r in range(pieces)]
    e = jnp.concatenate(parts, axis=1).astype(F32) * gain[...].astype(F32)
    mean_e = jnp.mean(e, axis=-1, keepdims=True)
    mean_ex = jnp.mean(e * xhat, axis=-1, keepdims=True)
    out[...] = (cot[...].astype(F32) + (e - mean_e - xhat * mean_ex) * inverse).astype(BF)


def input_grads(info, grad, tok, cot, gain, chunk):
    rows, width = grad.shape
    share = pl.BlockSpec((rows, width), lambda i, s: (s[1], 0))
    return call(
        functools.partial(input_body, chunk=chunk),
        "input_grad",
        (1,),
        [row_block(rows, width), share, share, fixed((1, width))],
        [row_block(rows, width)],
        [jax.ShapeDtypeStruct((rows, width), BF)],
        [],
        20 * grad.size,
        8 * grad.size,
    )(info, grad, tok, cot, gain[None])[0]


def layer_body(info, branch, tok, bias, out, *, chunk):
    for r in range(tok.shape[1] // chunk):
        at = slice(r * chunk, r * chunk + chunk)
        part = branch[:, lanes_of(info, chunk, r)].astype(F32)
        out[:, at] = (tok[:, at].astype(F32) + part + bias[:, at].astype(F32)).astype(BF)


def layer_rows(info, branch, tok, bias, chunk):
    rows, width = branch.shape
    return call(
        functools.partial(layer_body, chunk=chunk),
        "layer_out",
        (1,),
        [row_block(rows, width), pl.BlockSpec((rows, width), lambda i, s: (s[1], 0)), fixed((1, width))],
        [row_block(rows, width)],
        [jax.ShapeDtypeStruct((rows, width), BF)],
        [],
        4 * branch.size,
        6 * branch.size,
    )(info, branch, tok, bias[None])[0]


def norm_sums_body(info, grad, tok, gain_sum, shift_sum, *, chunk):
    xhat, _ = norm_parts(tok[...].astype(F32))

    @pl.when(pl.program_id(0) == 0)
    def _():
        gain_sum[...] = jnp.zeros_like(gain_sum)
        shift_sum[...] = jnp.zeros_like(shift_sum)

    for r in range(tok.shape[1] // chunk):
        at = slice(r * chunk, r * chunk + chunk)
        part = grad[:, lanes_of(info, chunk, r)].astype(F32)
        shift_sum[:, at] += jnp.sum(part, axis=0, keepdims=True)
        gain_sum[:, at] += jnp.sum(part * xhat[:, at], axis=0, keepdims=True)


def norm_sums(info, grad, tok, chunk):
    rows, width = grad.shape
    size = min(rows, 256)
    one = pl.BlockSpec((1, width), lambda i, s: (0, 0))
    return call(
        functools.partial(norm_sums_body, chunk=chunk),
        "norm_sums",
        (rows // size,),
        [row_block(size, width)] * 2,
        [one, one],
        [jax.ShapeDtypeStruct((1, width), F32)] * 2,
        [],
        20 * grad.size,
        4 * grad.size,
    )(info, grad, tok)


def body(tokens, cotangent, piece_ids, positions, norm_gain, norm_shift, in_proj, in_bias, out_proj, up_proj, up_bias, down_proj, out_bias):
    length, depth = tokens.shape
    width = in_bias.shape[1] // 2
    hidden_width = up_bias.shape[0] // 2
    f_count, z_count = lax.axis_size("fsdp"), lax.axis_size("tp")
    x_at, c_at, f_at = lax.axis_index("cx"), lax.axis_index("cc"), lax.axis_index("fsdp")
    square = f_count == 2
    chips = 2 * f_count
    chunk = depth // chips
    me = f_at * 2 + x_at if square else 0 * f_at
    info = jnp.stack([me, lax.axis_index("tp")]).astype(jnp.int32)

    other_core = lambda value: lax.ppermute(value, "cc", SWAP)
    by_x = lambda value: lax.ppermute(value, "cx", SWAP)
    by_y = lambda value: lax.ppermute(value, "fsdp", SWAP)

    def pick(value, index, size, axis):
        return lax.dynamic_slice_in_dim(value, index * size, size, axis)

    def in_order(mine, theirs, axis):
        return jnp.where(c_at == 0, jnp.concatenate([mine, theirs], axis), jnp.concatenate([theirs, mine], axis))

    def cut_attention(c):
        parts = [pick(in_proj[j], c, width, 1) for j in range(3)]
        return jnp.concatenate(parts + [pick(out_proj, c, width, 0).T], axis=1)

    def cut_hidden(c):
        return jnp.concatenate([pick(up_proj, c, hidden_width, 1), pick(down_proj, c, hidden_width, 0).T], axis=1)

    def gather(value):
        if not square:
            return lax.all_gather(value, ("fsdp", "cx"), axis=0, tiled=True)
        middle = value.shape[0] // 2
        from_x, from_y = by_x(value), by_y(value)
        far = [by_x(from_y[:middle]), by_y(from_x[middle:])]
        return jnp.concatenate([value, from_x, from_y] + far, axis=0)

    weights_a = gather(in_order(cut_attention(c_at), other_core(cut_attention(1 - c_at)), 0))
    small = jnp.stack([piece_ids, positions])
    small = jnp.concatenate([small, other_core(small)], axis=1)
    pieces, places = small[0], small[1]
    normed, cot, cot_sum = prepare(info, tokens, cotangent, norm_gain, norm_shift, chunk)
    normed = jnp.concatenate([normed, other_core(normed)], axis=0)
    cot = jnp.concatenate([cot, other_core(cot)], axis=0)
    weights_m = gather(in_order(cut_hidden(c_at), other_core(cut_hidden(1 - c_at)), 0))

    lane = jnp.arange(128, dtype=jnp.int32) % HD
    slot = (lane % (ROT // 2)).astype(F32)
    angles = places.astype(F32)[:, None] * (10000.0 ** (-2.0 * slot / ROT))[None, :]
    cos_part, sin_part = jnp.cos(angles), jnp.sin(angles)
    tables = (
        jnp.where(lane[None] < ROT, cos_part, 1.0),
        jnp.where(lane[None] < ROT // 2, -sin_part, 0.0),
        jnp.where((lane[None] >= ROT // 2) & (lane[None] < ROT), sin_part, 0.0),
    )
    bias_a = pick(in_bias, c_at, width, 1).reshape(1, 3 * width)
    bias_m = pick(up_bias, c_at, hidden_width, 0)[None]
    flags = (pieces.reshape(-1, RUN)[:, 0] > 0).astype(jnp.int32)
    scene = jnp.concatenate([jnp.stack([c_at * (length // RUN), x_at]).astype(jnp.int32), flags])

    queries, kv, grad_att = project(info, normed, cot, weights_a, bias_a, tables, width)
    kvx = lax.ppermute(kv, "cx", [(0, 1)])
    attended, stat = attend(scene, queries, grad_att, kv, kvx)
    active, grad_up, up_sum = hidden(info, normed, cot, weights_m, bias_m, hidden_width)

    def reduce_rows(left, right, x_first, name):
        if not square:
            whole = outer(info, left, right, (0, 0), chunk, name)
            return lax.psum_scatter(whole, ("fsdp", "cx"), scatter_dimension=0, tiled=True)
        near, far = (by_x, by_y) if x_first else (by_y, by_x)
        sent, kept = ((1, 2), (0, 2)) if x_first else ((2, 1), (0, 1))
        away = outer(info, left, right, sent, chunk, name)
        came = near(away)
        held = outer(info, left, right, kept, chunk, name)
        add = lambda a, b: (a.astype(F32) + b.astype(F32)).astype(BF)
        second = add(held[chunk:], came[chunk:])
        return add(add(held[:chunk], came[:chunk]), far(second))

    up_rows = reduce_rows(normed, grad_up, True, "up_grad")
    down_rows = reduce_rows(cot, active, False, "down_grad")
    out_rows = reduce_rows(cot, attended, False, "out_grad")

    ia, ib = 3, 1
    theirs = spread(info, attended, active, weights_a, weights_m, ia, ib, 1, length, None, "branch_away")
    ours = spread(info, attended, active, weights_a, weights_m, ia, ib, 0, length, other_core(theirs), "branch_here")
    branch = lax.psum_scatter(ours, "tp", scatter_dimension=0, tiled=True)
    layer_out = layer_rows(info, branch, tokens, out_bias, chunk)

    grad_q, grad_k, grad_v, away = attend_back(scene, queries, grad_att, stat, kv, kvx)
    other = lax.ppermute(away, "cx", [(1, 0)])
    grad_packed, in_sum = collect(info, grad_q, grad_k, grad_v, other, tables)
    theirs = spread(info, grad_packed, grad_up, weights_a, weights_m, 0, 0, 1, length, None, "normed_away")
    ours = spread(info, grad_packed, grad_up, weights_a, weights_m, 0, 0, 0, length, other_core(theirs), "normed_here")
    grad_normed = lax.psum_scatter(ours, "tp", scatter_dimension=0, tiled=True)
    gain_sum, shift_sum = norm_sums(info, ours, tokens, chunk)
    in_rows = reduce_rows(normed, grad_packed, True, "in_grad")
    input_grad = input_grads(info, grad_normed, tokens, cotangent, norm_gain, chunk)

    once = jnp.where(lax.axis_index("tp") == 0, cot_sum, 0.0)
    all_wide = jnp.concatenate([gain_sum, shift_sum, once], axis=1)
    narrow = jnp.concatenate([in_sum, up_sum], axis=1)
    wide_size = all_wide.shape[1]
    both = jnp.concatenate([all_wide, narrow], axis=1)
    if square:
        both = both + by_x(both)
        both = both + by_y(both)
    else:
        both = lax.psum(both, ("fsdp", "cx"))
    swapped = other_core(both)
    wide = both[:, :wide_size] + swapped[:, :wide_size]
    step = 1
    while step < z_count:
        wide = wide + lax.ppermute(wide, "tp", [(z, z ^ step) for z in range(z_count)])
        step *= 2
    gain_grad, shift_grad, outbias_grad = [wide[0, depth * j : depth * j + depth] for j in range(3)]
    narrow_pair = in_order(both[:, wide_size:], swapped[:, wide_size:], 0)
    inbias_grad = jnp.transpose(narrow_pair[:, : 3 * width].reshape(2, 3, width), (1, 0, 2)).reshape(3, 2 * width)
    upbias_grad = narrow_pair[:, 3 * width :].reshape(2 * hidden_width)

    def keep(rows):
        size = rows.shape[0] // 2
        mine, theirs = pick(rows, c_at, size, 0), pick(rows, 1 - c_at, size, 0)
        came = other_core(theirs)
        return jnp.where(c_at == 0, jnp.stack([mine, came]), jnp.stack([came, mine])).astype(F32)

    up_two, down_two, out_two, in_two = keep(up_rows), keep(down_rows), keep(out_rows), keep(in_rows)
    share = up_two.shape[1]
    upproj_grad = jnp.transpose(up_two, (1, 0, 2)).reshape(share, 2 * hidden_width)
    downproj_grad = jnp.transpose(down_two, (0, 2, 1)).reshape(2 * hidden_width, share)
    outproj_grad = jnp.transpose(out_two, (0, 2, 1)).reshape(2 * width, share)
    inproj_grad = jnp.transpose(in_two.reshape(2, share, 3, width), (2, 1, 0, 3)).reshape(3, share, 2 * width)
    return (
        layer_out,
        input_grad,
        gain_grad,
        shift_grad,
        inproj_grad,
        inbias_grad,
        outproj_grad,
        upproj_grad,
        upbias_grad,
        downproj_grad,
        outbias_grad,
    )


def solution(mesh):
    sizes = mesh.shape
    split = Mesh(
        mesh.devices.reshape(sizes["fsdp"], sizes["ctx"] // 2, 2, sizes["tp"]), ("fsdp", "cx", "cc", "tp")
    )
    group = ("fsdp", "cx", "cc")
    return jax.shard_map(
        body,
        mesh=split,
        in_specs=(
            P(group, None),
            P(group, None),
            P(group),
            P(group),
            P(),
            P(),
            P(None, group, "tp"),
            P(None, "tp"),
            P("tp", group),
            P(group, "tp"),
            P("tp"),
            P("tp", group),
            P(),
        ),
        out_specs=(
            P(group + ("tp",), None),
            P(group + ("tp",), None),
            P(),
            P(),
            P(None, group, "tp"),
            P(None, "tp"),
            P("tp", group),
            P(group, "tp"),
            P("tp"),
            P("tp", group),
            P(),
        ),
        check_vma=False,
    )
```

time: 1290 us -> 679 us (0.53)
  waiting for transfers between devices: 664 us -> 263 us
  Pallas kernels: 0 us -> 258 us
  matrix products: 222 us -> 0 us
  local copies, waits for them, and re-layouts: 165 us -> 59.9 us
  blocking collectives: 104 us -> 0 us
  other arithmetic: 101 us -> 41.2 us
  starting transfers between devices: 0.57 us -> 31.4 us
  loops' own time: 13.6 us -> 0 us
    reduce_scatter x8 -> x2, waiting for transfers between devices: 566 us -> 0.01 us  [the longest x1 0.01 us: body(): branch = lax.psum_scatter(ours, 'tp', scatter_dimension=0, tiled=True)]
    ppermute x0 -> x34, waiting for transfers between devices: none -> 263 us  [the longest x1 125 us: body(): other = lax.ppermute(away, 'cx', [(1, 0)])]
    pallas_call x0 -> x21, Pallas kernels: none -> 258 us  [the longest x8 66.3 us: outer(): call(outer_body, name, (count,), [pl.BlockSpec((rows, size), place), fixe...]
    dot_general x26 -> x0, matrix products: 222 us -> none  [the longest x3 38.8 us: dot_last(): lax.dot_general(matrix_a, matrix_b, (((matrix_a.ndim - 1,), (matrix_b.ndi...]
    all_gather x6 -> x0, waiting for transfers between devices: 95.6 us -> none  [the longest x1 44.3 us: body(): lax.all_gather(in_proj, ('fsdp', 'ctx'), axis=1, tiled=True)]
    psum x2 -> x0, blocking collectives: 93.1 us -> none  [the longest x1 51.5 us: body(): lax.psum((inbias_part, upbias_part), ('fsdp', 'ctx'))]
    reduce_sum x11 -> x0, other arithmetic: 41.5 us -> none  [the longest x2 18.5 us: online_update(): summed = summed * rescale + jnp.sum(weights, axis=-1)]
    reduce_or x16 -> x0, other arithmetic: 32.7 us -> none  [the longest x8 19.5 us: query_step(): jnp.any(visible_pairs)]
  transfers between devices with their start and end apart: 14 -> 36, of which waited for: 10 -> 13; matrix products, arithmetic and copies ran while one was open for 36% -> 13% of each run, Pallas kernels for 0% -> 30%
where the time goes in v1:
time: 679 us; the launch traced here: 669 us
  waiting for transfers between devices  263 us (39%)
  Pallas kernels  258 us (38%)
  local copies, waits for them, and re-layouts  59.9 us (9%)
  other arithmetic  41.2 us (6%)
  starting transfers between devices  31.4 us (5%)
  between operations  15.1 us (2%)
    ppermute x1, waiting for transfers between devices, body(): other = lax.ppermute(away, 'cx', [(1, 0)])  125 us
    ppermute x9, waiting for transfers between devices, body(): by_x = lambda value: lax.ppermute(value, 'cx', SWAP)  86.7 us
    pallas_call x8, Pallas kernels, outer(): call(outer_body, name, (count,), [pl.BlockSpec((rows, size), place), fixe...  66.3 us
    pallas_call x4, Pallas kernels, spread(): call(spread_body, name, (rows // size,), [at(wide_a), at(wide_b), fixed((...  50 us
    pallas_call x1, Pallas kernels, attend_back(): call(functools.partial(backward_body, pairs=pairs, cut=cut), 'attend_back...  37.5 us
    unnamed x80, local copies, waits for them, and re-layouts  34 us
    pallas_call x1, Pallas kernels, attend(): call(functools.partial(forward_body, pairs=pairs, cut=cut), 'attend', (ro...  27.7 us
    pallas_call x1, Pallas kernels, hidden(): call(hidden_body, 'hidden', (rows // size,), [spec, spec, fixed((depth, w...  25.6 us
  transfers between devices with their start and end apart: 36, of which 13 were waited for; matrix products, arithmetic and copies ran while one was open for 13% of the time, Pallas kernels for 30%

profile of v1, /device:TPU:0, one launch (start us, length us, event | category | flops | bytes accessed | tf_op | source)
XLA Modules:
  0.0 668.8 jit_solution(13265634956642048902)
XLA Ops:
  13.4 9.8 %normalize.1 = (bf16[1024,2048]{1,0:T(8,128)(2,1)}, bf16[1024,2048]{1,0:T(8,128)(2,1)}, f32[1,2048]{1,0:T(1,128)}) custom-call(s32[2]{0:T(128)} %pad_add_fusion.2.info, bf16[1024,2048]{1,0:T(8,128)(2,1)} %tok.7, bf16[1024,2048]{1,0:T(8,128)(2,1)} %cot.3, bf16[1,2048]{1,0:T(2,128)(2,1)} %broadcast_in_dim.49.gain, bf16[1,2048]{1,0:T(2,128)(2,1)} %broadcast_in_dim.50.shift), custom_call_target="tpu_custom_call" | custom-call | flops 20971520 | bytes 16777216 | tf_op jit(solution)/shard_map/normalize/pallas_call | solution.py:88
  26.2 7.9 %constant_dynamic-update-slice_fusion.8 = (bf16[2048,1024]{1,0:T(8,128)(2,1)}, bf16[512,1024]{1,0:T(8,128)(2,1)}) fusion(bf16[256,256]{1,0:T(8,128)(2,1)S(1)} %bitcast.76, bf16[256,256]{1,0:T(8,128)(2,1)S(1)} %get-tuple-element.95, bf16[256,256]{1,0:T(8,128)(2,1)S(1)} %get-tuple-element.110, bf16[256,256]{1,0:T(8,128)(2,1)S(1)} %copy-done.16, ...), kind=kLoop, calls=%fused_computation.47 | loop fusion | flops 11010047 | bytes 3145729
  40.0 10.7 %constant_dynamic-update-slice_fusion.13 = (bf16[2048,2048]{1,0:T(8,128)(2,1)}, bf16[512,2048]{1,0:T(8,128)(2,1)}) fusion(bf16[256,1024]{1,0:T(8,128)(2,1)S(1)} %bitcast.67, bf16[256,1024]{1,0:T(8,128)(2,1)S(1)} %get-tuple-element.80, bf16[256,2048]{1,0:T(8,128)(2,1)} %collective-permute-done.9, pred[]{:T(512)S(6)} %eq.7), kind=kLoop, calls=%fused_computation.52 | loop fusion | flops 13631487 | bytes 6291457
  51.1 9.8 %collective-permute-done.5 = bf16[512,1024]{1,0:T(8,128)(2,1)S(1)} collective-permute-done((bf16[512,1024]{1,0:T(8,128)(2,1)}, bf16[512,1024]{1,0:T(8,128)(2,1)S(1)}, u32[]{:S(2)}, u32[]{:S(2)}) %collective-permute-start.5) | collective-permute-done | bytes 1048608 | tf_op jit(solution)/shard_map/ppermute | solution.py:593
  62.9 7.1 %constant_dynamic-update-slice_fusion.1 = (bf16[2048,2048]{1,0:T(8,128)(2,1)}, bf16[2048,2048]{1,0:T(8,128)(2,1)}) fusion(bf16[1024,2048]{1,0:T(8,128)(2,1)S(1)} %copy-done.7, bf16[1024,2048]{1,0:T(8,128)(2,1)} %get-tuple-element.31), kind=kLoop, calls=%fused_computation.40 | loop fusion | bytes 16777216
  70.3 6.1 fusion
  77.5 42.8 %collective-permute-done.6 = bf16[256,1024]{1,0:T(8,128)(2,1)S(1)} collective-permute-done((bf16[256,1024]{1,0:T(8,128)(2,1)S(1)}, bf16[256,1024]{1,0:T(8,128)(2,1)S(1)}, u32[]{:S(2)}, u32[]{:S(2)}) %collective-permute-start.6) | collective-permute-done | bytes 524320 | tf_op jit(solution)/shard_map/ppermute | solution.py:592
  126.0 7.5 %collective-permute-done.7 = bf16[256,1024]{1,0:T(8,128)(2,1)S(1)} collective-permute-done((bf16[256,1024]{1,0:T(8,128)(2,1)S(1)}, bf16[256,1024]{1,0:T(8,128)(2,1)S(1)}, u32[]{:S(2)}, u32[]{:S(2)}) %collective-permute-start.7) | collective-permute-done | bytes 524320 | tf_op jit(solution)/shard_map/ppermute | solution.py:593
  145.3 5.5 constant_dynamic-update-slice_fusion.2.cot.left
  154.2 16.7 %project.1 = (bf16[2048,256]{1,0:T(8,128)(2,1)}, bf16[2048,512]{1,0:T(8,128)(2,1)}, bf16[2048,256]{1,0:T(8,128)(2,1)}) custom-call(s32[2]{0:T(128)} %pad_add_fusion.2.info, bf16[2048,2048]{1,0:T(8,128)(2,1)} %copy-done.2, bf16[2048,2048]{1,0:T(8,128)(2,1)} %copy-done.3, bf16[2048,1024]{1,0:T(8,128)(2,1)} %constant_dynamic-update-slice_fusion.4.weights.wa, ...), custom_call_target="tpu_custom_call" | custom-call | flops 8589934592 | bytes 25165824 | tf_op jit(solution)/shard_map/project/pallas_call | solution.py:126
  176.3 25.6 %hidden.1 = (bf16[2048,1024]{1,0:T(8,128)(2,1)}, bf16[2048,1024]{1,0:T(8,128)(2,1)}, f32[1,1024]{1,0:T(1,128)}) custom-call(s32[2]{0:T(128)} %pad_add_fusion.2.info, bf16[2048,2048]{1,0:T(8,128)(2,1)} %copy-done.2, bf16[2048,2048]{1,0:T(8,128)(2,1)} %copy-done.3, bf16[2048,2048]{1,0:T(8,128)(2,1)} %constant_dynamic-update-slice_fusion.9.up.down.wb, ...), custom_call_target="tpu_custom_call" | custom-call | flops 17179869184 | bytes 33554432 | tf_op jit(solution)/shard_map/hidden/pallas_call | solution.py:165
  201.9 15.1 %collective-permute-done.8.kx_ref.vx_ref = bf16[2048,512]{1,0:T(8,128)(2,1)S(1)} collective-permute-done((bf16[2048,512]{1,0:T(8,128)(2,1)}, bf16[2048,512]{1,0:T(8,128)(2,1)S(1)}, u32[]{:S(2)}, u32[]{:S(2)}) %collective-permute-start.8) | collective-permute-done | bytes 2097184 | tf_op jit(solution)/shard_map/ppermute | solution.py:640
  218.3 27.7 %attend.1 = (bf16[2048,256]{1,0:T(8,128)(2,1)}, f32[8,2048]{1,0:T(8,128)}) custom-call(s32[10]{0:T(128)} %pad_add_fusion.3.info, bf16[2048,256]{1,0:T(8,128)(2,1)} %get-tuple-element.32.q_ref, bf16[2048,256]{1,0:T(8,128)(2,1)} %get-tuple-element.33.do_ref, bf16[2048,512]{1,0:T(8,128)(2,1)} %get-tuple-element.34.k_ref.v_ref, ...), custom_call_target="tpu_custom_call" | custom-call | flops 40000000000 | bytes 7340032 | tf_op jit(solution)/shard_map/attend/pallas_call | solution.py:338
  246.0 10.8 %branch_away.1 = bf16[1024,2048]{1,0:T(8,128)(2,1)} custom-call(s32[2]{0:T(128)} %pad_add_fusion.2.info, bf16[2048,256]{1,0:T(8,128)(2,1)} %get-tuple-element.35.a.right, bf16[2048,1024]{1,0:T(8,128)(2,1)} %get-tuple-element.36.b.right, bf16[2048,1024]{1,0:T(8,128)(2,1)} %constant_dynamic-update-slice_fusion.4.weights.wa, ...), custom_call_target="tpu_custom_call" | custom-call | flops 5368709120 | bytes 12058624 | tf_op jit(solution)/shard_map/branch_away/pallas_call | solution.py:192
  256.8 7.4 %collective-permute-done.14.rest_0_ = bf16[1024,2048]{1,0:T(8,128)(2,1)S(1)} collective-permute-done((bf16[1024,2048]{1,0:T(8,128)(2,1)}, bf16[1024,2048]{1,0:T(8,128)(2,1)S(1)}, u32[]{:S(2)}, u32[]{:S(2)}) %collective-permute-start.14) | collective-permute-done | bytes 4194336 | tf_op jit(solution)/shard_map/ppermute | solution.py:591
  266.1 11.5 %branch_here.1 = bf16[1024,2048]{1,0:T(8,128)(2,1)} custom-call(s32[2]{0:T(128)} %pad_add_fusion.2.info, bf16[2048,256]{1,0:T(8,128)(2,1)} %get-tuple-element.35.a.right, bf16[2048,1024]{1,0:T(8,128)(2,1)} %get-tuple-element.36.b.right, bf16[2048,1024]{1,0:T(8,128)(2,1)} %constant_dynamic-update-slice_fusion.4.weights.wa, ...), custom_call_target="tpu_custom_call" | custom-call | flops 5368709120 | bytes 16252928 | tf_op jit(solution)/shard_map/branch_here/pallas_call | solution.py:192
  277.7 37.5 %attend_back.1 = (f32[2048,256]{1,0:T(8,128)}, f32[2048,256]{1,0:T(8,128)}, f32[2048,256]{1,0:T(8,128)}, bf16[2048,512]{1,0:T(8,128)(2,1)}) custom-call(s32[10]{0:T(128)} %pad_add_fusion.3.info, bf16[2048,256]{1,0:T(8,128)(2,1)} %get-tuple-element.32.q_ref, bf16[2048,256]{1,0:T(8,128)(2,1)} %get-tuple-element.33.do_ref, ...), custom_call_target="tpu_custom_call" | custom-call | flops 60000002048 | bytes 15728640 | tf_op jit(solution)/shard_map/attend_back/pallas_call | solution.py:446
  316.5 124.9 %collective-permute-done.15.other_k.other_v = bf16[2048,512]{1,0:T(8,128)(2,1)S(1)} collective-permute-done((bf16[2048,512]{1,0:T(8,128)(2,1)}, bf16[2048,512]{1,0:T(8,128)(2,1)S(1)}, u32[]{:S(2)}, u32[]{:S(2)}) %collective-permute-start.15) | collective-permute-done | bytes 2097184 | tf_op jit(solution)/shard_map/ppermute | solution.py:668
  442.7 8.3 %collect.1 = (bf16[2048,768]{1,0:T(8,128)(2,1)}, f32[1,768]{1,0:T(1,128)}) custom-call(s32[2]{0:T(128)} %pad_add_fusion.2.info, f32[2048,256]{1,0:T(8,128)} %get-tuple-element.38.dq, f32[2048,256]{1,0:T(8,128)} %get-tuple-element.39.dk, f32[2048,256]{1,0:T(8,128)} %get-tuple-element.40.dv, bf16[2048,512]{1,0:T(8,128)(2,1)} %copy-done.5, ...), custom_call_target="tpu_custom_call" | custom-call | flops 10485760 | bytes 15728640 | tf_op jit(solution)/shard_map/collect/pallas_call | solution.py:486
  451.0 13.7 %normed_away.1 = bf16[1024,2048]{1,0:T(8,128)(2,1)} custom-call(s32[2]{0:T(128)} %pad_add_fusion.2.info, bf16[2048,768]{1,0:T(8,128)(2,1)} %get-tuple-element.42.a.right, bf16[2048,1024]{1,0:T(8,128)(2,1)} %get-tuple-element.43.b.right, bf16[2048,1024]{1,0:T(8,128)(2,1)} %constant_dynamic-update-slice_fusion.4.weights.wa, ...), custom_call_target="tpu_custom_call" | custom-call | flops 7516192768 | bytes 15204352 | tf_op jit(solution)/shard_map/normed_away/pallas_call | solution.py:192
  465.3 9.4 %up_grad.3 = bf16[1024,1024]{1,0:T(8,128)(2,1)} custom-call(s32[2]{0:T(128)} %pad_add_fusion.2.info, bf16[2048,2048]{1,0:T(8,128)(2,1)} %copy-done.2, bf16[2048,1024]{1,0:T(8,128)(2,1)} %get-tuple-element.43.b.right), custom_call_target="tpu_custom_call" | custom-call | flops 4294967296 | bytes 10485760 | tf_op jit(solution)/shard_map/up_grad/pallas_call | solution.py:221
  474.7 9.4 %down_grad.3 = bf16[1024,1024]{1,0:T(8,128)(2,1)} custom-call(s32[2]{0:T(128)} %pad_add_fusion.2.info, bf16[2048,2048]{1,0:T(8,128)(2,1)} %copy-done.3, bf16[2048,1024]{1,0:T(8,128)(2,1)} %get-tuple-element.36.b.right), custom_call_target="tpu_custom_call" | custom-call | flops 4294967296 | bytes 10485760 | tf_op jit(solution)/shard_map/down_grad/pallas_call | solution.py:221
  485.8 14.0 %normed_here.1.grad = bf16[1024,2048]{1,0:T(8,128)(2,1)} custom-call(s32[2]{0:T(128)} %pad_add_fusion.2.info, bf16[2048,768]{1,0:T(8,128)(2,1)} %get-tuple-element.42.a.right, bf16[2048,1024]{1,0:T(8,128)(2,1)} %get-tuple-element.43.b.right, bf16[2048,1024]{1,0:T(8,128)(2,1)} %constant_dynamic-update-slice_fusion.4.weights.wa, ...), custom_call_target="tpu_custom_call" | custom-call | flops 7516192768 | bytes 19398656 | tf_op jit(solution)/shard_map/normed_here/pallas_call | solution.py:192
  499.9 9.6 %down_grad.2 = bf16[1024,1024]{1,0:T(8,128)(2,1)} custom-call(s32[2]{0:T(128)} %pad_add_fusion.2.info, bf16[2048,2048]{1,0:T(8,128)(2,1)} %copy-done.3, bf16[2048,1024]{1,0:T(8,128)(2,1)} %get-tuple-element.36.b.right), custom_call_target="tpu_custom_call" | custom-call | flops 4294967296 | bytes 10485760 | tf_op jit(solution)/shard_map/down_grad/pallas_call | solution.py:221
  509.5 5.8 out_grad.3
  515.3 9.3 %up_grad.2 = bf16[1024,1024]{1,0:T(8,128)(2,1)} custom-call(s32[2]{0:T(128)} %pad_add_fusion.2.info, bf16[2048,2048]{1,0:T(8,128)(2,1)} %copy-done.2, bf16[2048,1024]{1,0:T(8,128)(2,1)} %get-tuple-element.43.b.right), custom_call_target="tpu_custom_call" | custom-call | flops 4294967296 | bytes 10485760 | tf_op jit(solution)/shard_map/up_grad/pallas_call | solution.py:221
  524.7 5.9 out_grad.2
  530.5 8.4 %in_grad.3 = bf16[1024,768]{1,0:T(8,128)(2,1)} custom-call(s32[2]{0:T(128)} %pad_add_fusion.2.info, bf16[2048,2048]{1,0:T(8,128)(2,1)} %copy-done.2, bf16[2048,768]{1,0:T(8,128)(2,1)} %get-tuple-element.42.a.right), custom_call_target="tpu_custom_call" | custom-call | flops 3221225472 | bytes 8912896 | tf_op jit(solution)/shard_map/in_grad/pallas_call | solution.py:221
  549.8 31.6 %collective-permute-done.26 = bf16[512,256]{1,0:T(8,128)(2,1)S(1)} collective-permute-done((bf16[512,256]{1,0:T(8,128)(2,1)S(1)}, bf16[512,256]{1,0:T(8,128)(2,1)S(1)}, u32[]{:S(2)}, u32[]{:S(2)}) %collective-permute-start.26) | collective-permute-done | bytes 262176 | tf_op jit(solution)/shard_map/ppermute | solution.py:592
  585.7 8.5 %in_grad.2 = bf16[1024,768]{1,0:T(8,128)(2,1)} custom-call(s32[2]{0:T(128)} %pad_add_fusion.2.info, bf16[2048,2048]{1,0:T(8,128)(2,1)} %copy-done.2, bf16[2048,768]{1,0:T(8,128)(2,1)} %get-tuple-element.42.a.right), custom_call_target="tpu_custom_call" | custom-call | flops 3221225472 | bytes 8912896 | tf_op jit(solution)/shard_map/in_grad/pallas_call | solution.py:221
  599.8 9.0 %collective-permute-done.32 = bf16[512,1024]{1,0:T(8,128)(2,1)} collective-permute-done((bf16[512,1024]{1,0:T(8,128)(2,1)}, bf16[512,1024]{1,0:T(8,128)(2,1)}, u32[]{:S(2)}, u32[]{:S(2)}) %collective-permute-start.32) | collective-permute-done | bytes 1048608 | tf_op jit(solution)/shard_map/ppermute | solution.py:592
  617.9 7.7 %norm_sums.1 = (f32[1,2048]{1,0:T(1,128)}, f32[1,2048]{1,0:T(1,128)}) custom-call(s32[2]{0:T(128)} %pad_add_fusion.2.info, bf16[1024,2048]{1,0:T(8,128)(2,1)} %normed_here.1.grad, bf16[1024,2048]{1,0:T(8,128)(2,1)} %tok.7), custom_call_target="tpu_custom_call" | custom-call | flops 41943040 | bytes 8388608 | tf_op jit(solution)/shard_map/norm_sums/pallas_call | solution.py:566
  (215 shorter events, 118.8 us)
Async XLA Ops:
  7.2 645.6 %reduce-scatter.3.cloned.1.call-start = ((), (), s32[]{:S(2)}) async-start(), calls=%async_computation.2 | async-start | bytes 5242880 | tf_op jit(solution)/shard_map/reduce_scatter | solution.py:664
  11.1 15.1 %collective-permute-start.3 = (bf16[256,1024]{1,0:T(8,128)(2,1)}, bf16[256,1024]{1,0:T(8,128)(2,1)}, u32[]{:S(2)}, u32[]{:S(2)}) collective-permute-start(bf16[256,1024]{1,0:T(8,128)(2,1)} %pad_maximum_fusion.1), channel_id=1, source_target_pairs={{0,4},{4,0},{1,5},{5,1},{2,6},{6,2},{3,7},{7,3},{8,12},{12,8},{9,1... | collective-permute-start | bytes 1572872 | tf_op jit(solution)/shard_map/ppermute | solution.py:591
  23.2 119.0 %collective-permute-start.1 = (bf16[1024,2048]{1,0:T(8,128)(2,1)}, bf16[1024,2048]{1,0:T(8,128)(2,1)}, u32[]{:S(2)}, u32[]{:S(2)}) collective-permute-start(bf16[1024,2048]{1,0:T(8,128)(2,1)} %get-tuple-element.30), channel_id=1, source_target_pairs={{0,4},{4,0},{1,5},{5,1},{2,6},{6,2},{3,7},{7,3},{8,12},{12,8},{9,1... | collective-permute-start | bytes 12582920 | tf_op jit(solution)/shard_map/ppermute | solution.py:591
  25.6 12.8 %collective-permute-start.9 = (bf16[256,2048]{1,0:T(8,128)(2,1)}, bf16[256,2048]{1,0:T(8,128)(2,1)}, u32[]{:S(2)}, u32[]{:S(2)}) collective-permute-start(bf16[256,2048]{1,0:T(8,128)(2,1)} %pad_maximum_fusion), channel_id=1, source_target_pairs={{0,4},{4,0},{1,5},{5,1},{2,6},{6,2},{3,7},{7,3},{8,12},{12,8},{9,1... | collective-permute-start | bytes 3145736 | tf_op jit(solution)/shard_map/ppermute | solution.py:591
  25.6 119.7 %collective-permute-start.2 = (bf16[1024,2048]{1,0:T(8,128)(2,1)}, bf16[1024,2048]{1,0:T(8,128)(2,1)}, u32[]{:S(2)}, u32[]{:S(2)}) collective-permute-start(bf16[1024,2048]{1,0:T(8,128)(2,1)} %get-tuple-element.31), channel_id=1, source_target_pairs={{0,4},{4,0},{1,5},{5,1},{2,6},{6,2},{3,7},{7,3},{8,12},{12,8},{9,1... | collective-permute-start | bytes 12582920 | tf_op jit(solution)/shard_map/ppermute | solution.py:591
  34.1 26.8 %collective-permute-start.5 = (bf16[512,1024]{1,0:T(8,128)(2,1)}, bf16[512,1024]{1,0:T(8,128)(2,1)S(1)}, u32[]{:S(2)}, u32[]{:S(2)}) collective-permute-start(bf16[512,1024]{1,0:T(8,128)(2,1)} %get-tuple-element.74), channel_id=1, source_target_pairs={{0,16},{16,0},{1,17},{17,1},{2,18},{18,2},{3,19},{19,3},{4,20},{20... | collective-permute-start | bytes 3145736 | tf_op jit(solution)/shard_map/ppermute | solution.py:593
  36.8 13.9 %collective-permute-start = (s32[2,1024]{1,0:T(2,128)S(1)}, s32[2,1024]{1,0:T(2,128)S(1)}, u32[]{:S(2)}, u32[]{:S(2)}) collective-permute-start(s32[2,1024]{1,0:T(2,128)S(1)} %pad_add_fusion.1), channel_id=1, source_target_pairs={{0,4},{4,0},{1,5},{5,1},{2,6},{6,2},{3,7},{7,3},{8,12},{12,8},{9,1... | collective-permute-start | bytes 24584 | tf_op jit(solution)/shard_map/ppermute | solution.py:591
  38.4 31.7 %collective-permute-start.4 = (bf16[512,1024]{1,0:T(8,128)(2,1)}, bf16[512,1024]{1,0:T(8,128)(2,1)}, u32[]{:S(2)}, u32[]{:S(2)}) collective-permute-start(bf16[512,1024]{1,0:T(8,128)(2,1)} %get-tuple-element.74), channel_id=1, source_target_pairs={{0,8},{8,0},{1,9},{9,1},{2,10},{10,2},{3,11},{11,3},{4,12},{12,4},... | collective-permute-start | bytes 3145736 | tf_op jit(solution)/shard_map/ppermute | solution.py:592
  50.6 83.8 %collective-permute-start.11 = (bf16[512,2048]{1,0:T(8,128)(2,1)}, bf16[512,2048]{1,0:T(8,128)(2,1)S(1)}, u32[]{:S(2)}, u32[]{:S(2)}) collective-permute-start(bf16[512,2048]{1,0:T(8,128)(2,1)} %get-tuple-element.72), channel_id=1, source_target_pairs={{0,16},{16,0},{1,17},{17,1},{2,18},{18,2},{3,19},{19,3},{4,20},{20... | collective-permute-start | bytes 6291464 | tf_op jit(solution)/shard_map/ppermute | solution.py:593
  61.0 74.6 %collective-permute-start.10 = (bf16[512,2048]{1,0:T(8,128)(2,1)}, bf16[512,2048]{1,0:T(8,128)(2,1)}, u32[]{:S(2)}, u32[]{:S(2)}) collective-permute-start(bf16[512,2048]{1,0:T(8,128)(2,1)} %get-tuple-element.72), channel_id=1, source_target_pairs={{0,8},{8,0},{1,9},{9,1},{2,10},{10,2},{3,11},{11,3},{4,12},{12,4},... | collective-permute-start | bytes 6291464 | tf_op jit(solution)/shard_map/ppermute | solution.py:592
  70.1 50.2 %collective-permute-start.6 = (bf16[256,1024]{1,0:T(8,128)(2,1)S(1)}, bf16[256,1024]{1,0:T(8,128)(2,1)S(1)}, u32[]{:S(2)}, u32[]{:S(2)}) collective-permute-start(bf16[256,1024]{1,0:T(8,128)(2,1)S(1)} %slice.145), channel_id=1, source_target_pairs={{0,8},{8,0},{1,9},{9,1},{2,10},{10,2},{3,11},{11,3},{4,12},{12,4},... | collective-permute-start | bytes 1572872 | tf_op jit(solution)/shard_map/ppermute | solution.py:592
  120.3 13.3 %collective-permute-start.7 = (bf16[256,1024]{1,0:T(8,128)(2,1)S(1)}, bf16[256,1024]{1,0:T(8,128)(2,1)S(1)}, u32[]{:S(2)}, u32[]{:S(2)}) collective-permute-start(bf16[256,1024]{1,0:T(8,128)(2,1)S(1)} %slice.146), channel_id=1, source_target_pairs={{0,16},{16,0},{1,17},{17,1},{2,18},{18,2},{3,19},{19,3},{4,20},{20... | collective-permute-start | bytes 1572872 | tf_op jit(solution)/shard_map/ppermute | solution.py:593
  134.5 39.4 %collective-permute-start.12 = (bf16[256,2048]{1,0:T(8,128)(2,1)S(1)}, bf16[256,2048]{1,0:T(8,128)(2,1)S(1)}, u32[]{:S(2)}, u32[]{:S(2)}) collective-permute-start(bf16[256,2048]{1,0:T(8,128)(2,1)S(1)} %slice.148), channel_id=1, source_target_pairs={{0,8},{8,0},{1,9},{9,1},{2,10},{10,2},{3,11},{11,3},{4,12},{12,4},... | collective-permute-start | bytes 3145736 | tf_op jit(solution)/shard_map/ppermute | solution.py:592
  137.0 38.1 %collective-permute-start.13 = (bf16[256,2048]{1,0:T(8,128)(2,1)S(1)}, bf16[256,2048]{1,0:T(8,128)(2,1)S(1)}, u32[]{:S(2)}, u32[]{:S(2)}) collective-permute-start(bf16[256,2048]{1,0:T(8,128)(2,1)S(1)} %slice.149), channel_id=1, source_target_pairs={{0,16},{16,0},{1,17},{17,1},{2,18},{18,2},{3,19},{19,3},{4,20},{20... | collective-permute-start | bytes 3145736 | tf_op jit(solution)/shard_map/ppermute | solution.py:593
  170.9 46.1 %collective-permute-start.8 = (bf16[2048,512]{1,0:T(8,128)(2,1)}, bf16[2048,512]{1,0:T(8,128)(2,1)S(1)}, u32[]{:S(2)}, u32[]{:S(2)}) collective-permute-start(bf16[2048,512]{1,0:T(8,128)(2,1)} %get-tuple-element.34.k_ref.v_ref), channel_id=1, source_target_pairs={{0,8},{1,9},{2,10},{3,11},{4,12},{5,13},{6,14},{7,15},{16,24},{17,... | collective-permute-start | bytes 6291464 | tf_op jit(solution)/shard_map/ppermute | solution.py:640
  256.8 7.4 %collective-permute-start.14 = (bf16[1024,2048]{1,0:T(8,128)(2,1)}, bf16[1024,2048]{1,0:T(8,128)(2,1)S(1)}, u32[]{:S(2)}, u32[]{:S(2)}) collective-permute-start(bf16[1024,2048]{1,0:T(8,128)(2,1)} %branch_away.1), channel_id=1, source_target_pairs={{0,4},{4,0},{1,5},{5,1},{2,6},{6,2},{3,7},{7,3},{8,12},{12,8},{9,1... | collective-permute-start | bytes 12582920 | tf_op jit(solution)/shard_map/ppermute | solution.py:591
  277.7 378.7 %reduce-scatter.5.cloned.1.call-start = ((), (), s32[]{:S(2)}) async-start(), calls=%async_computation.3 | async-start | bytes 5242880 | tf_op jit(solution)/shard_map/reduce_scatter | solution.py:672
  315.2 126.2 %collective-permute-start.15 = (bf16[2048,512]{1,0:T(8,128)(2,1)}, bf16[2048,512]{1,0:T(8,128)(2,1)S(1)}, u32[]{:S(2)}, u32[]{:S(2)}) collective-permute-start(bf16[2048,512]{1,0:T(8,128)(2,1)} %get-tuple-element.41), channel_id=1, source_target_pairs={{8,0},{9,1},{10,2},{11,3},{12,4},{13,5},{14,6},{15,7},{24,16},{25,... | collective-permute-start | bytes 6291464 | tf_op jit(solution)/shard_map/ppermute | solution.py:668
  464.7 21.1 %collective-permute-start.16 = (bf16[1024,2048]{1,0:T(8,128)(2,1)}, bf16[1024,2048]{1,0:T(8,128)(2,1)}, u32[]{:S(2)}, u32[]{:S(2)}) collective-permute-start(bf16[1024,2048]{1,0:T(8,128)(2,1)} %normed_away.1), channel_id=1, source_target_pairs={{0,4},{4,0},{1,5},{5,1},{2,6},{6,2},{3,7},{7,3},{8,12},{12,8},{9,1... | collective-permute-start | bytes 12582920 | tf_op jit(solution)/shard_map/ppermute | solution.py:591
  474.7 70.8 %collective-permute-start.28 = (bf16[1024,1024]{1,0:T(8,128)(2,1)}, bf16[1024,1024]{1,0:T(8,128)(2,1)}, u32[]{:S(2)}, u32[]{:S(2)}) collective-permute-start(bf16[1024,1024]{1,0:T(8,128)(2,1)} %up_grad.3), channel_id=1, source_target_pairs={{0,8},{8,0},{1,9},{9,1},{2,10},{10,2},{3,11},{11,3},{4,12},{12,4},... | collective-permute-start | bytes 6291464 | tf_op jit(solution)/shard_map/ppermute | solution.py:592
  484.1 97.5 %collective-permute-start.31 = (bf16[1024,1024]{1,0:T(8,128)(2,1)}, bf16[1024,1024]{1,0:T(8,128)(2,1)S(1)}, u32[]{:S(2)}, u32[]{:S(2)}) collective-permute-start(bf16[1024,1024]{1,0:T(8,128)(2,1)} %down_grad.3), channel_id=1, source_target_pairs={{0,16},{16,0},{1,17},{17,1},{2,18},{18,2},{3,19},{19,3},{4,20},{20... | collective-permute-start | bytes 6291464 | tf_op jit(solution)/shard_map/ppermute | solution.py:593
  515.3 28.2 %collective-permute-start.25 = (bf16[1024,256]{1,0:T(8,128)(2,1)}, bf16[1024,256]{1,0:T(8,128)(2,1)S(1)}, u32[]{:S(2)}, u32[]{:S(2)}) collective-permute-start(bf16[1024,256]{1,0:T(8,128)(2,1)} %out_grad.3), channel_id=1, source_target_pairs={{0,16},{16,0},{1,17},{17,1},{2,18},{18,2},{3,19},{19,3},{4,20},{20... | collective-permute-start | bytes 1572872 | tf_op jit(solution)/shard_map/ppermute | solution.py:593
  538.9 55.2 %collective-permute-start.22 = (bf16[1024,768]{1,0:T(8,128)(2,1)}, bf16[1024,768]{1,0:T(8,128)(2,1)}, u32[]{:S(2)}, u32[]{:S(2)}) collective-permute-start(bf16[1024,768]{1,0:T(8,128)(2,1)} %in_grad.3), channel_id=1, source_target_pairs={{0,8},{8,0},{1,9},{9,1},{2,10},{10,2},{3,11},{11,3},{4,12},{12,4},... | collective-permute-start | bytes 4718600 | tf_op jit(solution)/shard_map/ppermute | solution.py:592
  543.6 37.7 %collective-permute-start.26 = (bf16[512,256]{1,0:T(8,128)(2,1)S(1)}, bf16[512,256]{1,0:T(8,128)(2,1)S(1)}, u32[]{:S(2)}, u32[]{:S(2)}) collective-permute-start(bf16[512,256]{1,0:T(8,128)(2,1)S(1)} %add_convert_fusion.10), channel_id=1, source_target_pairs={{0,8},{8,0},{1,9},{9,1},{2,10},{10,2},{3,11},{11,3},{4,12},{12,4},... | collective-permute-start | bytes 786440 | tf_op jit(solution)/shard_map/ppermute | solution.py:592
  548.0 49.6 %collective-permute-start.29 = (bf16[512,1024]{1,0:T(8,128)(2,1)}, bf16[512,1024]{1,0:T(8,128)(2,1)}, u32[]{:S(2)}, u32[]{:S(2)}) collective-permute-start(bf16[512,1024]{1,0:T(8,128)(2,1)} %add_convert_fusion.4), channel_id=1, source_target_pairs={{0,16},{16,0},{1,17},{17,1},{2,18},{18,2},{3,19},{19,3},{4,20},{20... | collective-permute-start | bytes 3145736 | tf_op jit(solution)/shard_map/ppermute | solution.py:593
  582.9 25.9 %collective-permute-start.32 = (bf16[512,1024]{1,0:T(8,128)(2,1)}, bf16[512,1024]{1,0:T(8,128)(2,1)}, u32[]{:S(2)}, u32[]{:S(2)}) collective-permute-start(bf16[512,1024]{1,0:T(8,128)(2,1)} %add_convert_fusion.1), channel_id=1, source_target_pairs={{0,8},{8,0},{1,9},{9,1},{2,10},{10,2},{3,11},{11,3},{4,12},{12,4},... | collective-permute-start | bytes 3145736 | tf_op jit(solution)/shard_map/ppermute | solution.py:592
  595.9 19.7 %collective-permute-start.23 = (bf16[512,768]{1,0:T(8,128)(2,1)S(1)}, bf16[512,768]{1,0:T(8,128)(2,1)S(1)}, u32[]{:S(2)}, u32[]{:S(2)}) collective-permute-start(bf16[512,768]{1,0:T(8,128)(2,1)S(1)} %add_convert_fusion.7), channel_id=1, source_target_pairs={{0,16},{16,0},{1,17},{17,1},{2,18},{18,2},{3,19},{19,3},{4,20},{20... | collective-permute-start | bytes 2359304 | tf_op jit(solution)/shard_map/ppermute | solution.py:593
  599.8 27.7 %collective-permute-start.30 = (bf16[256,1024]{1,0:T(8,128)(2,1)S(1)}, bf16[256,1024]{1,0:T(8,128)(2,1)S(1)}, u32[]{:S(2)}, u32[]{:S(2)}) collective-permute-start(bf16[256,1024]{1,0:T(8,128)(2,1)S(1)} %get-tuple-element.78), channel_id=1, source_target_pairs={{0,4},{4,0},{1,5},{5,1},{2,6},{6,2},{3,7},{7,3},{8,12},{12,8},{9,1... | collective-permute-start | bytes 1572872 | tf_op jit(solution)/shard_map/ppermute | solution.py:591
  610.8 22.1 %collective-permute-start.33 = (bf16[256,1024]{1,0:T(8,128)(2,1)S(1)}, bf16[256,1024]{1,0:T(8,128)(2,1)S(1)}, u32[]{:S(2)}, u32[]{:S(2)}) collective-permute-start(bf16[256,1024]{1,0:T(8,128)(2,1)S(1)} %get-tuple-element.76), channel_id=1, source_target_pairs={{0,4},{4,0},{1,5},{5,1},{2,6},{6,2},{3,7},{7,3},{8,12},{12,8},{9,1... | collective-permute-start | bytes 1572872 | tf_op jit(solution)/shard_map/ppermute | solution.py:591
  617.9 23.3 %collective-permute-start.24 = (bf16[256,768]{1,0:T(8,128)(2,1)}, bf16[256,768]{1,0:T(8,128)(2,1)S(1)}, u32[]{:S(2)}, u32[]{:S(2)}) collective-permute-start(bf16[256,768]{1,0:T(8,128)(2,1)} %get-tuple-element.84), channel_id=1, source_target_pairs={{0,4},{4,0},{1,5},{5,1},{2,6},{6,2},{3,7},{7,3},{8,12},{12,8},{9,1... | collective-permute-start | bytes 1179656 | tf_op jit(solution)/shard_map/ppermute | solution.py:591
  631.1 10.3 %collective-permute-start.18 = (f32[1,7936]{1,0:T(1,128)S(1)}, f32[1,7936]{1,0:T(1,128)S(1)}, u32[]{:S(2)}, u32[]{:S(2)}) collective-permute-start(f32[1,7936]{1,0:T(1,128)S(1)} %add.128), channel_id=1, source_target_pairs={{0,16},{16,0},{1,17},{17,1},{2,18},{18,2},{3,19},{19,3},{4,20},{20... | collective-permute-start | bytes 95240 | tf_op jit(solution)/shard_map/ppermute | solution.py:593
  647.4 4.8 collective-permute-start.21
  (35 other events, 304.6 us)
Sparse Core Ops, SparseCore 0:
  277.8 109.7 reduce-scatter.2
  500.0 76.9 reduce-scatter.4

commit v2 on v1

v2 whole, which is shorter than its diff:
```python
import functools
import math

import jax
import jax.numpy as jnp
from jax import lax
from jax.experimental import pallas as pl
from jax.experimental.pallas import tpu as pltpu
from jax.sharding import Mesh
from jax.sharding import PartitionSpec as P

HD = 64
ROT = 32
RUN = 256
EPS = 1e-05
NEG = -1e30
F32 = jnp.float32
BF = jnp.bfloat16
NN = (((1,), (0,)), ((), ()))
NT = (((1,), (1,)), ((), ()))
TN = (((0,), (0,)), ((), ()))
SWAP = [(0, 1), (1, 0)]
GELU_A = math.sqrt(2.0 / math.pi)
GELU_B = 0.044715
COST = 100.0


def dot(a, b, dims=NN):
    return lax.dot_general(a, b, dims, preferred_element_type=F32)


ANY = pl.BlockSpec(memory_space=pl.ANY)


def call(body, name, grid, in_specs, out_specs, out_shape, scratch, flops, moved, prefetch=1, vmem=60, collective=None):
    return pl.pallas_call(
        body,
        out_shape=out_shape,
        grid_spec=pltpu.PrefetchScalarGridSpec(
            num_scalar_prefetch=prefetch,
            grid=grid,
            in_specs=in_specs,
            out_specs=out_specs,
            scratch_shapes=scratch,
        ),
        compiler_params=pltpu.CompilerParams(
            vmem_limit_bytes=vmem << 20,
            dimension_semantics=("arbitrary",) * len(grid),
            collective_id=collective,
            has_side_effects=collective is not None,
        ),
        cost_estimate=pl.CostEstimate(flops=int(flops * COST), bytes_accessed=int(moved * COST), transcendentals=0),
        name=name,
    )


def row_block(size, width):
    return pl.BlockSpec((size, width), lambda i, s: (i, 0))


def fixed(shape, index=None):
    place = index or (0,) * len(shape)
    return pl.BlockSpec(shape, lambda i, s: place, pipeline_mode=pl.Buffered(1))


def norm_parts(rows):
    center = rows - jnp.mean(rows, axis=-1, keepdims=True)
    inverse = lax.rsqrt(jnp.mean(center * center, axis=-1, keepdims=True) + EPS)
    return center * inverse, inverse


def lanes_of(info, chunk, piece):
    return pl.ds(pl.multiple_of((piece ^ info[0]) * chunk, chunk), chunk)


def to_neighbour(source, target, sends, receives, n, axis, at):
    return pltpu.make_async_remote_copy(
        src_ref=source,
        dst_ref=target,
        send_sem=sends.at[n],
        recv_sem=receives.at[n],
        device_id={axis: at},
        device_id_type=pl.DeviceIdType.MESH,
    )


def begin_body(tok, cot, gain, shift, in_ref, out_ref, up_any, down_any, nrm, cot_out, wa, vm, cot_sum, chip_a, away_a, chip_m, away_m, up_ref, down_ref, nbuf, cbuf, loads, locals_, sends, receives, *, chunk, square, steps):
    i = pl.program_id(0)
    core, x, y = lax.axis_index("cc"), lax.axis_index("cx"), lax.axis_index("fsdp")
    shard = in_ref.shape[1]
    size, depth = tok.shape
    width, wide = chip_a.shape[1] // 4, chip_m.shape[1] // 2
    mine = pl.ds(pl.multiple_of(core * shard, shard), shard)
    rows = 2 * shard
    peers = [("cc", 1 - core)] + ([("cx", 1 - x), ("fsdp", 1 - y)] if square else [])

    load_up = pltpu.make_async_copy(up_any, up_ref, loads.at[0])
    load_down = pltpu.make_async_copy(down_any, down_ref, loads.at[1])
    swap_a = to_neighbour(away_a, chip_a.at[mine, :], sends, receives, 0, "cc", 1 - core)
    swap_m = to_neighbour(away_m, chip_m.at[mine, :], sends, receives, 1, "cc", 1 - core)
    keep_a = pltpu.make_async_copy(chip_a, wa.at[pl.ds(0, rows), :], locals_.at[0])
    keep_m = pltpu.make_async_copy(chip_m, vm, locals_.at[1])
    if square:
        to_x = to_neighbour(chip_a, wa.at[pl.ds(rows, rows), :], sends, receives, 2, "cx", 1 - x)
        to_y = to_neighbour(chip_a, wa.at[pl.ds(2 * rows, rows), :], sends, receives, 3, "fsdp", 1 - y)
        far_x = to_neighbour(
            wa.at[pl.ds(2 * rows, shard), :], wa.at[pl.ds(3 * rows, shard), :], sends, receives, 4, "cx", 1 - x
        )
        far_y = to_neighbour(
            wa.at[pl.ds(rows + shard, shard), :],
            wa.at[pl.ds(3 * rows + shard, shard), :],
            sends,
            receives,
            5,
            "fsdp",
            1 - y,
        )

    def row_copies(j):
        here = pl.ds(pl.multiple_of(j * size, size), size)
        there = pl.ds(pl.multiple_of((j + steps) * size, size), size)
        return [
            pltpu.make_async_copy(nbuf.at[j], nrm.at[here, :], locals_.at[2 + j]),
            pltpu.make_async_copy(cbuf.at[j], cot_out.at[here, :], locals_.at[2 + steps + j]),
            to_neighbour(nbuf.at[j], nrm.at[there, :], sends, receives, 6 + j, "cc", 1 - core),
            to_neighbour(cbuf.at[j], cot_out.at[there, :], sends, receives, 6 + steps + j, "cc", 1 - core),
        ]

    @pl.when(i == 0)
    def _():
        barrier = pltpu.get_barrier_semaphore()
        for axis, at in peers:
            pl.semaphore_signal(barrier, inc=1, device_id={axis: at}, device_id_type=pl.DeviceIdType.MESH)
        load_up.start()
        load_down.start()
        for target, c, at in ((chip_a, core, mine), (away_a, 1 - core, pl.ds(0, shard))):
            cut = pl.ds(pl.multiple_of(c * width, width), width)
            for j in range(3):
                target[at, width * j : width * j + width] = in_ref[j, :, cut]
            target[at, 3 * width :] = out_ref[cut, :].astype(F32).T.astype(BF)
        pl.semaphore_wait(barrier, len(peers))
        swap_a.start()
        load_up.wait()
        load_down.wait()
        for target, c, at in ((away_m, 1 - core, pl.ds(0, shard)), (chip_m, core, mine)):
            cut = pl.ds(pl.multiple_of(c * wide, wide), wide)
            target[at, :wide] = up_ref[:, cut]
            target[at, wide:] = down_ref[cut, :].astype(F32).T.astype(BF)
            if target is away_m:
                swap_m.start()
                swap_a.wait()
                if square:
                    to_x.start()
                    to_y.start()
                keep_a.start()
        cot_sum[...] = jnp.zeros_like(cot_sum)

    center, _ = norm_parts(tok[...].astype(F32))
    full = (center * gain[...].astype(F32)[None] + shift[...].astype(F32)[None]).astype(BF)
    cot_sum[...] += jnp.sum(cot[...].astype(F32), axis=0, keepdims=True)
    for r in range(depth // chunk):
        place = ((r // 2 + y) % 2) * 2 + (r % 2 + x) % 2 if square else r
        lanes = pl.ds(pl.multiple_of(place * chunk, chunk), chunk) if square else pl.ds(r * chunk, chunk)
        nbuf[i, :, lanes] = full[:, r * chunk : r * chunk + chunk]
        cbuf[i, :, lanes] = cot[:, r * chunk : r * chunk + chunk]
    for copy in row_copies(i):
        copy.start()

    @pl.when(i == steps - 1)
    def _():
        swap_m.wait()
        keep_m.start()
        if square:
            to_y.wait()
            far_x.start()
            to_x.wait()
            far_y.start()
        keep_a.wait()
        keep_m.wait()

        def finish(j, c):
            for copy in row_copies(j):
                copy.wait()
            return c

        lax.fori_loop(0, steps, finish, 0)
        if square:
            far_x.wait()
            far_y.wait()


def begin(tokens, cot, gain, shift, in_proj, out_proj, up_proj, down_proj, chunk, square):
    length, depth = tokens.shape
    steps = 4
    size = length // steps
    shard = in_proj.shape[1]
    width, wide = in_proj.shape[2] // 2, up_proj.shape[1] // 2
    block = pl.BlockSpec((size, depth), lambda i: (i, 0))
    whole = lambda shape: pl.BlockSpec(shape, lambda i: (0,) * len(shape), pipeline_mode=pl.Buffered(1))
    rows = 8 * shard if square else 2 * shard
    return call(
        functools.partial(begin_body, chunk=chunk, square=square, steps=steps),
        "begin",
        (steps,),
        [block, block, whole((depth,)), whole((depth,)), whole(in_proj.shape), whole(out_proj.shape), ANY, ANY],
        [ANY, ANY, ANY, ANY, pl.BlockSpec((1, depth), lambda i: (0, 0))],
        [
            jax.ShapeDtypeStruct((2 * length, depth), BF),
            jax.ShapeDtypeStruct((2 * length, depth), BF),
            jax.ShapeDtypeStruct((rows, 4 * width), BF),
            jax.ShapeDtypeStruct((2 * shard, 2 * wide), BF),
            jax.ShapeDtypeStruct((1, depth), F32),
        ],
        [
            pltpu.VMEM((2 * shard, 4 * width), BF),
            pltpu.VMEM((shard, 4 * width), BF),
            pltpu.VMEM((2 * shard, 2 * wide), BF),
            pltpu.VMEM((shard, 2 * wide), BF),
            pltpu.VMEM(up_proj.shape, BF),
            pltpu.VMEM(down_proj.shape, BF),
            pltpu.VMEM((steps, size, depth), BF),
            pltpu.VMEM((steps, size, depth), BF),
            pltpu.SemaphoreType.DMA((2,)),
            pltpu.SemaphoreType.DMA((2 + 2 * steps,)),
            pltpu.SemaphoreType.DMA((6 + 2 * steps,)),
            pltpu.SemaphoreType.DMA((6 + 2 * steps,)),
        ],
        10 * tokens.size,
        16 * tokens.size,
        prefetch=0,
        collective=0,
    )(tokens, cot, gain, shift, in_proj, out_proj, up_proj, down_proj)


def rotary_tables(cos_rows, sin_rows):
    one = jnp.ones((HD - ROT, cos_rows.shape[1]), F32)
    none = jnp.zeros((HD - ROT, cos_rows.shape[1]), F32)
    few = jnp.zeros_like(cos_rows)
    return (
        jnp.concatenate([cos_rows, cos_rows, one] * 2, axis=0).T,
        jnp.concatenate([-sin_rows, few, none] * 2, axis=0).T,
        jnp.concatenate([few, sin_rows, none] * 2, axis=0).T,
    )


def turn(values, cos_part, down, up):
    return (
        values * cos_part
        + pltpu.roll(values, 128 - ROT // 2, 1) * down
        + pltpu.roll(values, ROT // 2, 1) * up
    )


def stay(shape):
    return pl.BlockSpec(shape, lambda i, s: (0,) * len(shape))


def piece_copies(pieces, columns, target, sems):
    copies, at = [], 0
    for n, piece in enumerate(pieces):
        count = piece.shape[0]
        copies.append(
            pltpu.make_async_copy(piece.at[:, columns], target.at[pl.ds(at, count), :], sems.at[n])
        )
        at += count
    return copies


def place_pieces(*jobs):
    copies = [copy for job in jobs for copy in piece_copies(*job)]
    for copy in copies:
        copy.start()
    for copy in copies:
        copy.wait()


def move_sems(pieces):
    return pltpu.SemaphoreType.DMA((len(pieces),))


def project_body(info, nrm, cot, weights, bias, cos_t, sin_t, q_out, kv_out, do_out, send, *, width):
    packed = dot(nrm[...], weights[:, : 3 * width]) + bias[...].astype(F32)
    do = dot(cot[...], weights[:, 3 * width :]).astype(BF)
    c, d, u = rotary_tables(cos_t[...], sin_t[...])
    low = []
    for p in range(2 * width // 128):
        low.append(turn(packed[:, 128 * p : 128 * p + 128], c, d, u).astype(BF))
    pairs = width // 128
    queries = jnp.concatenate(low[:pairs], axis=1)
    keys = jnp.concatenate(low[pairs:], axis=1)
    values = packed[:, 2 * width :].astype(BF)
    q_out[...] = queries
    kv_out[:, :width] = keys
    kv_out[:, width:] = values
    do_out[...] = do
    part = width // 2

    @pl.when(info[3] == 0)
    def _():
        send[:, :part] = keys[:, :part]
        send[:, part:] = values[:, :part]

    @pl.when(info[3] != 0)
    def _():
        send[:, :part] = queries[:, part:]
        send[:, part:] = do[:, part:]


def project(info, normed, cot, weights, bias, tables, width):
    rows, depth = normed.shape
    size = min(rows, 256)
    table = pl.BlockSpec((ROT // 2, size), lambda i, s: (0, i))
    return call(
        functools.partial(project_body, width=width),
        "project",
        (rows // size,),
        [row_block(size, depth)] * 2 + [fixed((depth, 4 * width)), fixed((1, 3 * width)), table, table],
        [row_block(size, width), row_block(size, 2 * width), row_block(size, width), row_block(size, width)],
        [jax.ShapeDtypeStruct((rows, n * width), BF) for n in (1, 2, 1, 1)],
        [],
        2 * rows * depth * 4 * width,
        2 * (2 * rows * depth + depth * 4 * width + 5 * rows * width),
    )(info, normed, cot, weights, bias, *tables)


def hidden_body(info, nrm, cot, bias, *rest, width, count):
    pieces, (act_out, grad_out, sum_out, weights, sems) = rest[:count], rest[count:]

    @pl.when(pl.program_id(0) == 0)
    def _():
        place_pieces((pieces, slice(0, 2 * width), weights, sems))
        sum_out[...] = jnp.zeros_like(sum_out)

    u = dot(nrm[...], weights[:, :width]) + bias[...].astype(F32)
    g = dot(cot[...], weights[:, width:])
    square = u * u
    t = jnp.tanh(GELU_A * (u + GELU_B * square * u))
    half = 0.5 * (1.0 + t)
    act_out[...] = (u * half).astype(BF)
    slope = half + 0.5 * u * (1.0 - t * t) * (GELU_A * (1.0 + 3.0 * GELU_B * square))
    low = (g * slope).astype(BF)
    grad_out[...] = low
    sum_out[...] += jnp.sum(low.astype(F32), axis=0, keepdims=True)


def hidden(info, normed, cot, pieces, bias, width):
    rows, depth = normed.shape
    size = min(rows, 256)
    return call(
        functools.partial(hidden_body, width=width, count=len(pieces)),
        "hidden",
        (rows // size,),
        [row_block(size, depth)] * 2 + [fixed((1, width))] + [ANY] * len(pieces),
        [row_block(size, width), row_block(size, width), stay((1, width))],
        [jax.ShapeDtypeStruct((rows, width), BF)] * 2 + [jax.ShapeDtypeStruct((1, width), F32)],
        [pltpu.VMEM((depth, 2 * width), BF), move_sems(pieces)],
        4 * rows * depth * width,
        2 * (2 * rows * depth + 2 * depth * width + 2 * rows * width),
    )(info, normed, cot, bias, *pieces)


def spread_body(a, b, *rest, counts, columns, sums, per):
    na, nb = counts
    wa, wb = rest[:na], rest[na : na + nb]
    rest = rest[na + nb :]
    normed = rest[:sums]
    out = rest[sums]
    totals = rest[sums + 1 : 3 * sums + 1]
    hold_a, hold_b, sem_a, sem_b, outgoing, incoming, send_sems, recv_sems = rest[3 * sums + 1 :]
    i = pl.program_id(0)
    core = lax.axis_index("cc")

    def copy(j):
        return pltpu.make_async_remote_copy(
            src_ref=outgoing.at[j],
            dst_ref=incoming.at[j],
            send_sem=send_sems.at[j],
            recv_sem=recv_sems.at[j],
            device_id={"cc": 1 - core},
            device_id_type=pl.DeviceIdType.MESH,
        )

    @pl.when(i == 0)
    def _():
        barrier = pltpu.get_barrier_semaphore()
        pl.semaphore_signal(barrier, inc=1, device_id={"cc": 1 - core}, device_id_type=pl.DeviceIdType.MESH)
        place_pieces((wa, columns[0], hold_a, sem_a), (wb, columns[1], hold_b, sem_b))
        pl.semaphore_wait(barrier, 1)
        for total in totals:
            total[...] = jnp.zeros_like(total)

    total = dot(a[...], hold_a[...], NT) + dot(b[...], hold_b[...], NT)

    @pl.when(i < per)
    def _():
        outgoing[i] = total.astype(BF)
        copy(i).start()

    @pl.when(i >= per)
    def _():
        copy(i - per).wait()
        full = total + incoming[i - per].astype(F32)
        out[...] = full.astype(BF)
        if sums:
            totals[0][...] += jnp.sum(full * normed[0][...].astype(F32), axis=0, keepdims=True)
            totals[1][...] += jnp.sum(full, axis=0, keepdims=True)


def spread(a, b, wa, wb, ca, cb, depth, name, collective, normed=()):
    rows = a.shape[0] // 2
    size = min(rows, 256)
    per = rows // size
    at = lambda width: pl.BlockSpec((size, width), lambda i: ((i + per) % (2 * per), 0))
    later = pl.BlockSpec((size, depth), lambda i: (jnp.maximum(i - per, 0), 0))
    one = pl.BlockSpec((1, depth), lambda i: (0, 0))
    wide_a, wide_b = a.shape[1], b.shape[1]
    count = len(normed)
    return call(
        functools.partial(
            spread_body,
            counts=(len(wa), len(wb)),
            columns=(slice(ca, ca + wide_a), slice(cb, cb + wide_b)),
            sums=count,
            per=per,
        ),
        name,
        (2 * per,),
        [at(wide_a), at(wide_b)] + [ANY] * (len(wa) + len(wb)) + [later] * count,
        [later] + [one] * (2 * count),
        [jax.ShapeDtypeStruct((rows, depth), BF)] + [jax.ShapeDtypeStruct((1, depth), F32)] * (2 * count),
        [
            pltpu.VMEM((depth, wide_a), BF),
            pltpu.VMEM((depth, wide_b), BF),
            move_sems(wa),
            move_sems(wb),
            pltpu.VMEM((per, size, depth), BF),
            pltpu.VMEM((per, size, depth), BF),
            pltpu.SemaphoreType.DMA((per,)),
            pltpu.SemaphoreType.DMA((per,)),
        ],
        4 * rows * depth * (wide_a + wide_b),
        2 * (2 * rows + depth) * (wide_a + wide_b) + 2 * rows * depth,
        prefetch=0,
        collective=collective,
    )(a, b, *wa, *wb, *normed)


def outer_body(info, left_n, left_c, right_n, right_c, *rest, steps, out_steps):
    i = pl.program_id(0)
    outs = rest[:-3]
    hold_n, hold_c, sems = rest[-3:]
    load_n = pltpu.make_async_copy(right_n, hold_n, sems.at[0])
    load_c = pltpu.make_async_copy(right_c, hold_c, sems.at[1])

    @pl.when(i == 0)
    def _():
        load_n.start()
        load_c.start()
        load_n.wait()

    @pl.when(i == steps)
    def _():
        load_c.wait()

    for n, (start, stop) in enumerate(out_steps):
        left, right = (left_n, hold_n) if stop <= steps else (left_c, hold_c)

        @pl.when((i >= start) & (i < stop))
        def _(left=left, right=right, out=outs[n]):
            out[...] = dot(left[...], right[...], TN).astype(BF)


def outer(info, normed, cot, right_n, right_c, groups_n, groups_c, chunk, name):
    rows = right_n.shape[0]
    wide_n, wide_c = right_n.shape[1], right_c.shape[1]
    size = min(chunk, 512)
    per = chunk // size
    order_n = [block for group in groups_n for block in group]
    order_c = [block for group in groups_c for block in group]
    steps = len(order_n) * per

    def column(order, offset):
        def place(i, s):
            at = jnp.clip(i - offset, 0, steps - 1)
            block = order[-1]
            for k in range(len(order) - 1):
                block = jnp.where(at // per == k, order[k], block)
            return (0, block * per + at % per)

        return pl.BlockSpec((rows, size), place)

    out_specs, out_shapes, out_steps = [], [], []
    start = 0
    for groups, wide in ((groups_n, wide_n), (groups_c, wide_c)):
        for group in groups:
            count = len(group) * per
            out_specs.append(
                pl.BlockSpec((size, wide), lambda i, s, start=start, count=count: (jnp.clip(i - start, 0, count - 1), 0))
            )
            out_shapes.append(jax.ShapeDtypeStruct((count * size, wide), BF))
            out_steps.append((start, start + count))
            start += count
    return call(
        functools.partial(outer_body, steps=steps, out_steps=tuple(out_steps)),
        name,
        (2 * steps,),
        [column(order_n, 0), column(order_c, steps), ANY, ANY],
        out_specs,
        out_shapes,
        [pltpu.VMEM((rows, wide_n), BF), pltpu.VMEM((rows, wide_c), BF), pltpu.SemaphoreType.DMA((2,))],
        2 * rows * steps * size * (wide_n + wide_c),
        2 * (2 * rows * steps * size + (rows + steps * size) * (wide_n + wide_c)),
    )(info, normed, cot, right_n, right_c)


def head_masks(block, scale):
    lane = lax.broadcasted_iota(jnp.int32, block.shape, 1)
    v = block.astype(F32) * scale
    return (jnp.where(lane < HD, v, 0.0).astype(BF), jnp.where(lane < HD, 0.0, v).astype(BF))


def own_mask(flag, width):
    kk = lax.broadcasted_iota(jnp.int32, (RUN, width), 0)
    qq = lax.broadcasted_iota(jnp.int32, (RUN, width), 1)
    return kk <= qq + flag * RUN


def each_prefix(here, half, runs, work):
    size = runs // 2
    while size:

        @pl.when((here & size) != 0)
        def _(size=size):
            low = here & ((runs - 1) & ~(2 * size - 1))
            work(pl.multiple_of((low ^ half) * RUN, RUN), size * RUN)

        size //= 2


def softmax_blocks(state, heads, k_r, vt_r, qm, start, size, mask=None):
    acc, ml = state

    def score(n):
        p, h = divmod(n, 2)
        s = dot(k_r[pl.ds(start, size), 128 * p : 128 * p + 128], qm[p][h], NT)
        return s if mask is None else jnp.where(mask, s, NEG)

    def rest(n, s):
        top = jnp.max(s, axis=0, keepdims=True)
        rows = slice(HD * n, HD * n + HD)
        vb = vt_r[rows, pl.ds(start, size)]
        m = ml[n : n + 1, :]
        new = jnp.maximum(m, top)
        alpha = jnp.exp(m - new)
        e = jnp.exp(s - new)
        ml[n : n + 1, :] = new
        ml[heads + n : heads + n + 1, :] = ml[heads + n : heads + n + 1, :] * alpha + jnp.sum(e, axis=0, keepdims=True)
        acc[rows, :] = acc[rows, :] * alpha + dot(vb, e.astype(BF))

    s = score(0)
    for n in range(heads):
        following = score(n + 1) if n + 1 < heads else None
        rest(n, s)
        s = following


def start_state(acc, ml, heads):
    acc[...] = jnp.zeros_like(acc)
    ml[:heads, :] = jnp.full((heads, ml.shape[1]), NEG, F32)
    ml[heads:, :] = jnp.zeros((heads, ml.shape[1]), F32)


def finish_state(acc, ml, heads, n):
    l = ml[heads + n : heads + n + 1, :]
    return acc[HD * n : HD * n + HD, :] / l, ml[n : n + 1, :] + jnp.log(l)


def query_masks(block, scale):
    return [head_masks(block[:, 128 * p : 128 * p + 128], scale) for p in range(block.shape[1] // 128)]


SCALE = 1.0 / math.sqrt(HD)


def local_body(info, q_ref, k_ref, v_ref, out_ref, lse_ref, vt, acc, ml, *, heads):
    i = pl.program_id(0)
    half = info[0]
    runs = k_ref.shape[0] // RUN

    @pl.when(i == 0)
    def _():
        vt[...] = v_ref[...].astype(F32).T.astype(BF)

    qm = query_masks(q_ref[...], SCALE)
    start_state(acc, ml, heads)
    work = lambda start, size, mask=None: softmax_blocks((acc, ml), heads, k_ref, vt, qm, start, size, mask)
    work(pl.multiple_of(i * RUN, RUN), RUN, own_mask(info[2 + i], q_ref.shape[0]))
    each_prefix(i ^ half, half, runs, work)
    for n in range(heads):
        out_ref[HD * n : HD * n + HD, :], lse_ref[n : n + 1, :] = finish_state(acc, ml, heads, n)


def attend_local(info, q, kv):
    rows, width = q.shape
    heads = width // HD
    columns = lambda count: pl.BlockSpec((count, RUN), lambda i, s: (0, i))
    return call(
        functools.partial(local_body, heads=heads),
        "attend_local",
        (rows // RUN,),
        [row_block(RUN, width), fixed((rows, width)), fixed((rows, width), (0, 1))],
        [columns(width), columns(heads)],
        [jax.ShapeDtypeStruct((width, rows), F32), jax.ShapeDtypeStruct((heads, rows), F32)],
        [pltpu.VMEM((width, rows), BF), pltpu.VMEM((width, RUN), F32), pltpu.VMEM((2 * heads, RUN), F32)],
        25e9,
        14 * rows * width,
    )(info, q, kv, kv)


def cross_body(info, q_ref, came_ref, came0, came1, k_ref, v_ref, out_ref, lse_ref, keys, vt, acc, ml, *, heads, cut):
    late = info[1] > 0

    @pl.when(pl.program_id(0) == 0)
    def _():
        keys[...] = jnp.where(late, came0[...], k_ref[...])
        vt[...] = jnp.where(late, came1[...], v_ref[...]).astype(F32).T.astype(BF)

    qm = query_masks(jnp.where(late, q_ref[...], came_ref[...]), SCALE)
    start_state(acc, ml, heads)
    for j in range(keys.shape[0] // cut):
        softmax_blocks((acc, ml), heads, keys, vt, qm, j * cut, cut)
    for n in range(heads):
        out, lse_ref[n : n + 1, :] = finish_state(acc, ml, heads, n)
        out_ref[HD * n : HD * n + HD, :] = out.astype(BF)


def cross_specs(rows, part):
    own = lambda i, s: (i, 1 - s[1])
    return (
        pl.BlockSpec((RUN, part), own),
        pl.BlockSpec((RUN, part), lambda i, s: (i, 0)),
        fixed((rows, part)),
        fixed((rows, part), (0, 1)),
        pl.BlockSpec((rows, part), lambda i, s: (0, 1 - s[1])),
        pl.BlockSpec((rows, part), lambda i, s: (0, 3 - s[1])),
    )


def attend_cross(info, q, came, kv):
    rows, part = q.shape[0], q.shape[1] // 2
    heads = part // HD
    query, came_block, came0, came1, key, value = cross_specs(rows, part)
    columns = lambda count: pl.BlockSpec((count, RUN), lambda i, s: (0, i))
    return call(
        functools.partial(cross_body, heads=heads, cut=min(rows, 1024)),
        "attend_cross",
        (rows // RUN,),
        [query, came_block, came0, came1, key, value],
        [columns(part), columns(heads)],
        [jax.ShapeDtypeStruct((part, rows), BF), jax.ShapeDtypeStruct((heads, rows), F32)],
        [
            pltpu.VMEM((rows, part), BF),
            pltpu.VMEM((part, rows), BF),
            pltpu.VMEM((part, RUN), F32),
            pltpu.VMEM((2 * heads, RUN), F32),
        ],
        15e9,
        14 * rows * part,
    )(info, q, came, came, came, kv, kv)


def merge_body(info, local, lse_local, mine, lse_mine, came, lse_came, do_ref, att_ref, stat_ref, *, heads):
    late = info[1] > 0
    part = heads // 2
    size = do_ref.shape[0]
    do_t = do_ref[...].astype(F32).T
    outs = []
    for n in range(heads):
        other, lse_other, m = (mine, lse_mine, n) if n < part else (came, lse_came, n - part)
        rows = slice(HD * n, HD * n + HD)
        ours = lse_local[n : n + 1, :]
        theirs = jnp.where(late, lse_other[m : m + 1, :], jnp.full((1, size), NEG, F32))
        top = jnp.maximum(ours, theirs)
        a, b = jnp.exp(ours - top), jnp.exp(theirs - top)
        total = a + b
        o = (local[rows, :] * a + other[HD * m : HD * m + HD, :].astype(F32) * b) / total
        outs.append(o)
        stat_ref[n : n + 1, :] = top + jnp.log(total)
        stat_ref[heads + n : heads + n + 1, :] = jnp.sum(o * do_t[rows, :], axis=0, keepdims=True)
    att_ref[...] = jnp.concatenate(outs, axis=0).T.astype(BF)


def merge(info, local, lse_local, mine, lse_mine, came, lse_came, do):
    rows, width = do.shape
    heads = width // HD
    size = min(rows, 512)
    columns = lambda count: pl.BlockSpec((count, size), lambda i, s: (0, i))
    return call(
        functools.partial(merge_body, heads=heads),
        "merge",
        (rows // size,),
        [columns(width), columns(heads)] + [columns(width // 2), columns(heads // 2)] * 2 + [row_block(size, width)],
        [row_block(size, width), columns(2 * heads)],
        [jax.ShapeDtypeStruct((rows, width), BF), jax.ShapeDtypeStruct((2 * heads, rows), F32)],
        [],
        20 * rows * width,
        10 * rows * width,
    )(info, local, lse_local, mine, lse_mine, came, lse_came, do)


def gradient_blocks(heads, k_r, v_r, kt_r, dk_r, dv_r, dqt, qm, dm, stat, start, size, mask=None):
    def products(n):
        p, h = divmod(n, 2)
        lanes = slice(128 * p, 128 * p + 128)
        return (
            dot(k_r[pl.ds(start, size), lanes], qm[p][h], NT),
            dot(v_r[pl.ds(start, size), lanes], dm[p][h], NT),
        )

    def rest(n, s, g):
        p, h = divmod(n, 2)
        e = jnp.exp(s - stat[n : n + 1, :])
        if mask is not None:
            e = jnp.where(mask, e, 0.0)
        ds = (e * (g - stat[heads + n : heads + n + 1, :])).astype(BF)
        rows = slice(HD * n, HD * n + HD)
        dqt[rows, :] += dot(kt_r[rows, pl.ds(start, size)], ds)
        return dot(ds, qm[p][h]), dot(e.astype(BF), dm[p][h])

    now = products(0)
    before = None
    for n in range(heads):
        following = products(n + 1) if n + 1 < heads else None
        grads = rest(n, *now)
        now = following
        if n % 2:
            lanes = slice(HD * (n - 1), HD * (n + 1))
            dk_r[pl.ds(start, size), lanes] += before[0] + grads[0]
            dv_r[pl.ds(start, size), lanes] += before[1] + grads[1]
        before = grads


def local_back_body(info, q_ref, do_ref, stat_ref, k_ref, v_ref, dqx, dkx, dvx, came_q, came_k, came_v, cos_t, sin_t, out, sums, kt, dqt, dk, dv, *, heads):
    i = pl.program_id(0)
    half = info[0]
    late = info[1] > 0
    runs = k_ref.shape[0] // RUN
    width = HD * heads
    part = width // 2

    @pl.when(i == 0)
    def _():
        kt[...] = k_ref[...].astype(F32).T.astype(BF)

    @pl.when((i == 0) & late)
    def _():
        dk[...] = jnp.zeros_like(dk)
        dv[...] = jnp.zeros_like(dv)

    @pl.when((i == 0) & jnp.logical_not(late))
    def _():
        dk[:, :part] = came_k[...].astype(F32)
        dk[:, part:] = dkx[...]
        dv[:, :part] = came_v[...].astype(F32)
        dv[:, part:] = dvx[...]

    qm = query_masks(q_ref[...], SCALE)
    dm = query_masks(do_ref[...], 1.0)
    dqt[...] = jnp.zeros_like(dqt)

    def work(start, size, mask=None):
        gradient_blocks(heads, k_ref, v_ref, kt, dk, dv, dqt, qm, dm, stat_ref, start, size, mask)

    work(pl.multiple_of(i * RUN, RUN), RUN, own_mask(info[2 + i], q_ref.shape[0]))
    each_prefix(i ^ half, half, runs, work)
    zero = jnp.zeros((q_ref.shape[0], part), F32)
    more = jnp.concatenate(
        [jnp.where(late, dqx[...], zero), jnp.where(late, came_q[...].astype(F32), zero)], axis=1
    )
    found = (dqt[...] * SCALE).T + more
    rows = pl.ds(pl.multiple_of(i * RUN, RUN), RUN)
    c, d, u = rotary_tables(cos_t[:, rows], -sin_t[:, rows])
    for p in range(width // 128):
        lanes = slice(128 * p, 128 * p + 128)
        out[rows, lanes] = turn(found[:, lanes], c, d, u).astype(BF)

    @pl.when(i == pl.num_programs(0) - 1)
    def _():
        def step(j, c):
            at = pl.ds(pl.multiple_of(j * RUN, RUN), RUN)
            c2, d2, u2 = rotary_tables(cos_t[:, at], -sin_t[:, at])
            for p in range(width // 128):
                lanes = slice(128 * p, 128 * p + 128)
                shifted = slice(width + 128 * p, width + 128 * p + 128)
                out[at, shifted] = turn(dk[at, lanes], c2, d2, u2).astype(BF)
            out[at, 2 * width :] = dv[at, :].astype(BF)
            return c + jnp.sum(out[at, :].astype(F32), axis=0, keepdims=True)

        sums[...] = lax.fori_loop(0, runs, step, jnp.zeros((1, 3 * width), F32))


def back_local(info, q, do, stat, kv, cross, came, tables):
    rows, width = q.shape
    heads = width // HD
    part = width // 2
    blk = row_block(RUN, width)
    few = row_block(RUN, part)
    return call(
        functools.partial(local_back_body, heads=heads),
        "back_local",
        (rows // RUN,),
        [
            blk,
            blk,
            pl.BlockSpec((2 * heads, RUN), lambda i, s: (0, i)),
            fixed((rows, width)),
            fixed((rows, width), (0, 1)),
            few,
            fixed((rows, part)),
            fixed((rows, part)),
            few,
            fixed((rows, part)),
            fixed((rows, part), (0, 1)),
            fixed((ROT // 2, rows)),
            fixed((ROT // 2, rows)),
        ],
        [stay((rows, 3 * width)), stay((1, 3 * width))],
        [jax.ShapeDtypeStruct((rows, 3 * width), BF), jax.ShapeDtypeStruct((1, 3 * width), F32)],
        [
            pltpu.VMEM((width, rows), BF),
            pltpu.VMEM((width, RUN), F32),
            pltpu.VMEM((rows, width), F32),
            pltpu.VMEM((rows, width), F32),
        ],
        40e9,
        20 * rows * width,
    )(info, q, do, stat, kv, kv, *cross, came, came, came, *tables)


def cross_back_body(info, q_ref, do_ref, came_q, came_do, came0, came1, k_ref, v_ref, stat_ref, dq_ref, dk_ref, dv_ref, send, keys, values, kt, dqt, *, heads, cut):
    late = info[1] > 0
    i = pl.program_id(0)
    part = HD * heads

    @pl.when(i == 0)
    def _():
        chosen = jnp.where(late, came0[...], k_ref[...])
        keys[...] = chosen
        kt[...] = chosen.astype(F32).T.astype(BF)
        values[...] = jnp.where(late, came1[...], v_ref[...])
        dk_ref[...] = jnp.zeros_like(dk_ref)
        dv_ref[...] = jnp.zeros_like(dv_ref)

    qm = query_masks(jnp.where(late, q_ref[...], came_q[...]), SCALE)
    dm = query_masks(jnp.where(late, do_ref[...], came_do[...]), 1.0)
    dqt[...] = jnp.zeros_like(dqt)
    for j in range(keys.shape[0] // cut):
        gradient_blocks(heads, keys, values, kt, dk_ref, dv_ref, dqt, qm, dm, stat_ref, j * cut, cut)
    found = (dqt[...] * SCALE).T
    dq_ref[...] = found
    rows = pl.ds(pl.multiple_of(i * RUN, RUN), RUN)

    @pl.when(jnp.logical_not(late))
    def _():
        send[rows, :part] = found.astype(BF)
        send[rows, part:] = found.astype(BF)

    @pl.when(late & (i == pl.num_programs(0) - 1))
    def _():
        send[:, :part] = dk_ref[...].astype(BF)
        send[:, part:] = dv_ref[...].astype(BF)


def back_cross(info, q, do, came, kv, stat):
    rows, part = q.shape[0], q.shape[1] // 2
    heads = part // HD
    query, came_block, came0, came1, key, value = cross_specs(rows, part)
    acc = jax.ShapeDtypeStruct((rows, part), F32)
    return call(
        functools.partial(cross_back_body, heads=heads, cut=min(rows, 1024)),
        "back_cross",
        (rows // RUN,),
        [
            query,
            query,
            came_block,
            pl.BlockSpec((RUN, part), lambda i, s: (i, 1)),
            came0,
            came1,
            key,
            value,
            pl.BlockSpec((2 * heads, RUN), lambda i, s: (0, i)),
        ],
        [row_block(RUN, part), stay((rows, part)), stay((rows, part)), stay((rows, 2 * part))],
        [acc, acc, acc, jax.ShapeDtypeStruct((rows, 2 * part), BF)],
        [
            pltpu.VMEM((rows, part), BF),
            pltpu.VMEM((rows, part), BF),
            pltpu.VMEM((part, rows), BF),
            pltpu.VMEM((part, RUN), F32),
        ],
        25e9,
        20 * rows * part,
    )(info, q, do, came, came, came, came, kv, kv, stat)


def input_body(info, grad, tok, cot, gain, out, *, chunk):
    xhat, inverse = norm_parts(tok[...].astype(F32))
    parts = [grad[:, lanes_of(info, chunk, r)] for r in range(tok.shape[1] // chunk)]
    e = jnp.concatenate(parts, axis=1).astype(F32) * gain[...].astype(F32)
    mean_e = jnp.mean(e, axis=-1, keepdims=True)
    mean_ex = jnp.mean(e * xhat, axis=-1, keepdims=True)
    out[...] = (cot[...].astype(F32) + (e - mean_e - xhat * mean_ex) * inverse).astype(BF)


def input_grads(info, grad, tok, cot, gain, chunk):
    rows, width = grad.shape
    steps = 4
    size = rows // steps
    share = pl.BlockSpec((size, width), lambda i, s: (s[1] * steps + i, 0))
    return call(
        functools.partial(input_body, chunk=chunk),
        "input_grad",
        (steps,),
        [row_block(size, width), share, share, fixed((1, width))],
        [row_block(size, width)],
        [jax.ShapeDtypeStruct((rows, width), BF)],
        [],
        20 * rows * width,
        8 * rows * width,
    )(info, grad, tok, cot, gain[None])[0]


def layer_body(info, branch, tok, bias, out, *, chunk):
    for r in range(tok.shape[1] // chunk):
        at = slice(r * chunk, r * chunk + chunk)
        part = branch[:, lanes_of(info, chunk, r)].astype(F32)
        out[:, at] = (tok[:, at].astype(F32) + part + bias[:, at].astype(F32)).astype(BF)


def layer_rows(info, branch, tok, bias, chunk):
    rows, width = branch.shape
    return call(
        functools.partial(layer_body, chunk=chunk),
        "layer_out",
        (1,),
        [row_block(rows, width), pl.BlockSpec((rows, width), lambda i, s: (s[1], 0)), fixed((1, width))],
        [row_block(rows, width)],
        [jax.ShapeDtypeStruct((rows, width), BF)],
        [],
        4 * branch.size,
        6 * branch.size,
    )(info, branch, tok, bias[None])[0]


def body(tokens, cotangent, piece_ids, positions, norm_gain, norm_shift, in_proj, in_bias, out_proj, up_proj, up_bias, down_proj, out_bias):
    length, depth = tokens.shape
    width = in_bias.shape[1] // 2
    hidden_width = up_bias.shape[0] // 2
    f_count, z_count = lax.axis_size("fsdp"), lax.axis_size("tp")
    x_at, c_at, f_at = lax.axis_index("cx"), lax.axis_index("cc"), lax.axis_index("fsdp")
    square = f_count == 2
    chips = 2 * f_count
    chunk = depth // chips
    me = f_at * 2 + x_at if square else 0 * f_at
    info = jnp.stack([me, lax.axis_index("tp"), c_at, x_at]).astype(jnp.int32)

    other_core = lambda value: lax.ppermute(value, "cc", SWAP)
    by_x = lambda value: lax.ppermute(value, "cx", SWAP)
    by_y = lambda value: lax.ppermute(value, "fsdp", SWAP)

    def pick(value, index, size, axis):
        return lax.dynamic_slice_in_dim(value, index * size, size, axis)

    def in_order(mine, theirs, axis):
        return jnp.where(c_at == 0, jnp.concatenate([mine, theirs], axis), jnp.concatenate([theirs, mine], axis))

    def after(value, *earlier):
        return lax.optimization_barrier((value,) + earlier)[0]

    shard = in_proj.shape[1]
    normed, cot, weights_a, value_m, cot_sum = begin(
        tokens, cotangent, norm_gain, norm_shift, in_proj, out_proj, up_proj, down_proj, chunk, square
    )
    if not square:
        weights_a = lax.all_gather(weights_a, ("fsdp", "cx"), axis=0, tiled=True)
        weights_m = [lax.all_gather(value_m, ("fsdp", "cx"), axis=0, tiled=True)]
    small = jnp.stack([piece_ids, positions])
    small = jnp.concatenate([small, other_core(small)], axis=1)
    pieces, places = small[0], small[1]

    frequency = 10000.0 ** (-2.0 * jnp.arange(ROT // 2, dtype=F32) / ROT)
    angles = frequency[:, None] * places.astype(F32)[None, :]
    tables = (jnp.cos(angles), jnp.sin(angles))
    bias_a = pick(in_bias, c_at, width, 1).reshape(1, 3 * width)
    bias_m = pick(up_bias, c_at, hidden_width, 0)[None]
    flags = (pieces.reshape(-1, RUN)[:, 0] > 0).astype(jnp.int32)
    scene = jnp.concatenate([jnp.stack([c_at * (length // RUN), x_at]).astype(jnp.int32), flags])

    if square:
        x_first, y_m = by_x(value_m[:shard]), by_y(value_m)
    queries, kv, grad_att, send = project(info, normed, cot, weights_a, bias_a, tables, width)
    came = by_x(send)
    local, lse_local = attend_local(scene, after(queries, x_first) if square else queries, kv)
    mine, lse_mine = attend_cross(scene, after(queries, local), came, kv)
    if square:
        x_second = by_x(after(value_m[shard:], local))
        y_back = by_y(x_first)
    forward_x = lambda value: lax.ppermute(value, "cx", [(0, 1)])
    attended, stat = merge(
        scene,
        after(local, x_second) if square else local,
        lse_local,
        mine,
        lse_mine,
        forward_x(mine),
        forward_x(lse_mine),
        grad_att,
    )
    heads = width // HD
    part = heads // 2
    stat_early = jnp.concatenate([stat[:part], stat[heads : heads + part]], axis=0)
    stat_late = jnp.concatenate([stat[part:heads], stat[heads + part :]], axis=0)
    stat_cross = jnp.where(x_at == 1, stat_early, lax.ppermute(stat_late, "cx", [(1, 0)]))
    if square:
        weights_m = [value_m, x_first, x_second, y_m, y_back, by_x(after(y_m[shard:], stat_cross))]
    *cross, outgoing = back_cross(
        scene, after(queries, y_back) if square else queries, grad_att, came, kv, stat_cross
    )
    returned = by_x(outgoing)
    active, grad_up, up_sum = hidden(info, normed, cot, weights_m, after(bias_m, outgoing), hidden_width)

    def scatter(value):
        return lax.psum_scatter(value, ("fsdp", "cx"), scatter_dimension=0, tiled=True)

    def grads_of(after_this, right_n, right_c, name):
        left = after(normed, after_this)
        if square:
            return outer(info, left, cot, right_n, right_c, ((1, 3), (2, 0)), ((2, 3), (1, 0)), chunk, name)
        every = (tuple(range(chips)),)
        return outer(info, left, cot, right_n, right_c, every, every, chunk, name)

    def add(*values):
        return functools.reduce(lambda a, b: a + b, [value.astype(F32) for value in values])

    columns = (3 * width, hidden_width)
    (ours,) = spread(after(attended, active), active, [weights_a], weights_m, *columns, depth, "branch", 1)
    branch = lax.psum_scatter(ours, "tp", scatter_dimension=0, tiled=True)
    hidden_grads = grads_of(ours, grad_up, active, "hidden_grads")
    last = hidden_grads[-1]
    if square:
        up_away, up_held, down_away, down_held = hidden_grads
        up_came, down_came = by_x(up_away), by_y(down_away)
    grad_packed, in_sum = back_local(scene, after(queries, last), grad_att, stat, kv, cross, returned, tables)
    ours, gain_part, shift_part = spread(
        after(grad_packed, up_came, down_came) if square else grad_packed, grad_up, [weights_a], weights_m, 0, 0, depth, "normed_grad", 2, (normed,)
    )
    grad_normed = lax.psum_scatter(ours, "tp", scatter_dimension=0, tiled=True)
    if square:
        up_pass = add(after(up_held[:chunk], ours), up_came[chunk:]).astype(BF)
        down_pass = add(after(down_held[:chunk], ours), down_came[chunk:]).astype(BF)
        up_last, down_last = by_y(up_pass), by_x(down_pass)
    packed_grads = grads_of([up_pass, down_pass] if square else ours, grad_packed, attended, "packed_grads")
    def keep(rows):
        size = rows.shape[0] // 2
        mine, theirs = pick(rows, c_at, size, 0).astype(F32), pick(rows, 1 - c_at, size, 0).astype(BF)
        came = other_core(theirs).astype(F32)
        return jnp.where(c_at == 0, jnp.stack([mine, came]), jnp.stack([came, mine]))

    def hidden_outputs(up_rows, down_rows):
        up_two, down_two = keep(up_rows), keep(down_rows)
        return (
            jnp.transpose(up_two, (1, 0, 2)).reshape(shard, 2 * hidden_width),
            jnp.transpose(down_two, (0, 2, 1)).reshape(2 * hidden_width, shard),
        )

    def packed_outputs(in_rows, out_rows):
        in_two, out_two = keep(in_rows), keep(out_rows)
        return (
            jnp.transpose(in_two.reshape(2, shard, 3, width), (2, 1, 0, 3)).reshape(3, shard, 2 * width),
            jnp.transpose(out_two, (0, 2, 1)).reshape(2 * width, shard),
        )

    if square:
        in_away, in_held, out_away, out_held = packed_grads
        in_came, out_came = by_x(in_away), by_y(out_away)
        layer_out = layer_rows(info, after(branch, in_away, up_last, down_last), tokens, out_bias, chunk)
        up_rows = add(after(up_held[chunk:], layer_out), up_came[:chunk], up_last)
        down_rows = add(after(down_held[chunk:], layer_out), down_came[:chunk], down_last)
        upproj_grad, downproj_grad = hidden_outputs(up_rows, down_rows)
        in_pass = add(after(in_held[:chunk], upproj_grad, downproj_grad), in_came[chunk:]).astype(BF)
        out_pass = add(after(out_held[:chunk], layer_out), out_came[chunk:]).astype(BF)
        in_last, out_last = by_y(in_pass), by_x(out_pass)
        in_rows = add(in_held[chunk:], in_came[:chunk], in_last)
        out_rows = add(out_held[chunk:], out_came[:chunk], out_last)
        inproj_grad, outproj_grad = packed_outputs(in_rows, out_rows)
    else:
        upproj_grad, downproj_grad = hidden_outputs(*[scatter(value) for value in hidden_grads])
        inproj_grad, outproj_grad = packed_outputs(*[scatter(value) for value in packed_grads])
        layer_out = layer_rows(info, branch, tokens, out_bias, chunk)
    input_grad = input_grads(info, grad_normed, tokens, cotangent, norm_gain, chunk)

    def to_plain(row):
        if not square:
            return row
        return jnp.concatenate([pick(row, r ^ me, chunk, 1) for r in range(chips)], axis=1)

    shift_sum = to_plain(shift_part)
    gain_sum = (to_plain(gain_part) - shift_sum * norm_shift.astype(F32)[None]) / norm_gain.astype(F32)[None]
    once = jnp.where(lax.axis_index("tp") == 0, cot_sum, 0.0)
    all_wide = jnp.concatenate([gain_sum, shift_sum, once], axis=1)
    narrow = jnp.concatenate([in_sum, up_sum], axis=1)
    wide_size = all_wide.shape[1]
    both = jnp.concatenate([all_wide, narrow], axis=1)
    if square:
        both = both + by_x(both)
        both = both + by_y(both)
    else:
        both = lax.psum(both, ("fsdp", "cx"))
    swapped = other_core(both)
    wide = both[:, :wide_size] + swapped[:, :wide_size]
    step = 1
    while step < z_count:
        wide = wide + lax.ppermute(wide, "tp", [(z, z ^ step) for z in range(z_count)])
        step *= 2
    gain_grad, shift_grad, outbias_grad = [wide[0, depth * j : depth * j + depth] for j in range(3)]
    narrow_pair = in_order(both[:, wide_size:], swapped[:, wide_size:], 0)
    inbias_grad = jnp.transpose(narrow_pair[:, : 3 * width].reshape(2, 3, width), (1, 0, 2)).reshape(3, 2 * width)
    upbias_grad = narrow_pair[:, 3 * width :].reshape(2 * hidden_width)

    return (
        layer_out,
        input_grad,
        gain_grad,
        shift_grad,
        inproj_grad,
        inbias_grad,
        outproj_grad,
        upproj_grad,
        upbias_grad,
        downproj_grad,
        outbias_grad,
    )


def solution(mesh):
    sizes = mesh.shape
    split = Mesh(
        mesh.devices.reshape(sizes["fsdp"], sizes["ctx"] // 2, 2, sizes["tp"]), ("fsdp", "cx", "cc", "tp")
    )
    group = ("fsdp", "cx", "cc")
    return jax.shard_map(
        body,
        mesh=split,
        in_specs=(
            P(group, None),
            P(group, None),
            P(group),
            P(group),
            P(),
            P(),
            P(None, group, "tp"),
            P(None, "tp"),
            P("tp", group),
            P(group, "tp"),
            P("tp"),
            P("tp", group),
            P(),
        ),
        out_specs=(
            P(group + ("tp",), None),
            P(group + ("tp",), None),
            P(),
            P(),
            P(None, group, "tp"),
            P(None, "tp"),
            P("tp", group),
            P(group, "tp"),
            P("tp"),
            P("tp", group),
            P(),
        ),
        check_vma=False,
    )
```

time: 679 us -> 475 us (0.70)
  waiting for transfers between devices: 263 us -> 51 us
  Pallas kernels: 258 us -> 308 us
  local copies, waits for them, and re-layouts: 59.9 us -> 32.7 us
  other arithmetic: 41.2 us -> 22.9 us
  starting transfers between devices: 31.4 us -> 40.2 us
    ppermute x2 -> x3, waiting for transfers between devices: 140 us -> 6.68 us  [the longest x2 6.68 us: body(): forward_x = lambda value: lax.ppermute(value, 'cx', [(0, 1)])]
    ppermute x9 -> x10, waiting for transfers between devices: 86.7 us -> 8.05 us  [body(): by_x = lambda value: lax.ppermute(value, 'cx', SWAP)]
    pallas_call x19 -> x12, Pallas kernels: 238 us -> 287 us  [the longest x2 46.3 us: outer(): call(functools.partial(outer_body, steps=steps, out_steps=tuple(out_steps...]
    unnamed x80 -> x62, local copies, waits for them, and re-layouts: 34 us -> 7.52 us
    unnamed x5 -> x1, other arithmetic: 18.6 us -> 0.02 us
    ppermute x2 -> x3, starting transfers between devices: 4.34 us -> 16.5 us  [the longest x1 11.3 us: body(): lax.ppermute(stat_late, 'cx', [(1, 0)])]
    concatenate x4 -> x0, local copies, waits for them, and re-layouts: 10.5 us -> none  [the longest x1 5.49 us: body(): cot = jnp.concatenate([cot, other_core(cot)], axis=0)]
    slice x5 -> x7, local copies, waits for them, and re-layouts: 3.76 us -> 12 us  [the longest x1 3.1 us: body(): x_second = by_x(after(value_m[shard:], local))]
  transfers between devices with their start and end apart: 36 -> 30, of which waited for: 13 -> 9; matrix products, arithmetic and copies ran while one was open for 13% -> 11% of each run, Pallas kernels for 30% -> 64%
where the time goes in v2:
time: 475 us; the launch traced here: 470 us
  Pallas kernels  308 us (65%)
  waiting for transfers between devices  51 us (11%)
  starting transfers between devices  40.2 us (8%)
  local copies, waits for them, and re-layouts  32.7 us (7%)
  other arithmetic  22.9 us (5%)
  between operations  14.9 us (3%)
    pallas_call x2, Pallas kernels, outer(): call(functools.partial(outer_body, steps=steps, out_steps=tuple(out_steps...  46.3 us
    pallas_call x1, Pallas kernels, begin(): call(functools.partial(begin_body, chunk=chunk, square=square, steps=step...  45 us
    pallas_call x2, Pallas kernels, spread(): call(functools.partial(spread_body, counts=(len(wa), len(wb)), columns=(s...  44.8 us
    pallas_call x1, Pallas kernels, back_local(): call(functools.partial(local_back_body, heads=heads), 'back_local', (rows...  41.8 us
    ppermute x7, waiting for transfers between devices, body(): by_y = lambda value: lax.ppermute(value, 'fsdp', SWAP)  30.4 us
    pallas_call x1, Pallas kernels, back_cross(): call(functools.partial(cross_back_body, heads=heads, cut=min(rows, 1024))...  27.1 us
    pallas_call x1, Pallas kernels, attend_local(): call(functools.partial(local_body, heads=heads), 'attend_local', (rows //...  26.1 us
    pallas_call x1, Pallas kernels, hidden(): call(functools.partial(hidden_body, width=width, count=len(pieces)), 'hid...  25.9 us
  transfers between devices with their start and end apart: 30, of which 9 were waited for; matrix products, arithmetic and copies ran while one was open for 11% of the time, Pallas kernels for 64%

profile of v2, /device:TPU:0, one launch (start us, length us, event | category | flops | bytes accessed | tf_op | source)
XLA Modules:
  0.0 470.0 jit_solution(4843324655370659952)
XLA Ops:
  8.5 45.0 %begin.1 = (bf16[2048,2048]{1,0:T(8,128)(2,1)}, bf16[2048,2048]{1,0:T(8,128)(2,1)}, bf16[2048,1024]{1,0:T(8,128)(2,1)}, bf16[512,2048]{1,0:T(8,128)(2,1)}, f32[1,2048]{1,0:T(1,128)}) custom-call(bf16[1024,2048]{1,0:T(8,128)(2,1)} %tok.5, bf16[1024,2048]{1,0:T(8,128)(2,1)} %cot.3, bf16[2048]{0:T(1024)(128)(2,1)} %gain.1, bf16[2048]{0:T(1024)(128)(2,1)} %shift.1, ...), custom_call_target="tpu_custom_call" | custom-call | flops 2097152000 | bytes 3355443200 | tf_op jit(solution)/shard_map/begin/pallas_call | solution.py:201
  55.1 3.1 fusion.8
  61.8 17.3 %project.1 = (bf16[2048,256]{1,0:T(8,128)(2,1)}, bf16[2048,512]{1,0:T(8,128)(2,1)}, bf16[2048,256]{1,0:T(8,128)(2,1)}, bf16[2048,256]{1,0:T(8,128)(2,1)}) custom-call(s32[4]{0:T(128)} %pad_add_fusion.2.info, bf16[2048,2048]{1,0:T(8,128)(2,1)} %get-tuple-element.104.nrm.left_n.rest_7_, bf16[2048,2048]{1,0:T(8,128)(2,1)} %get-tuple-element.66.cot.left_c, ...), custom_call_target="tpu_custom_call" | custom-call | flops 858993459200 | bytes 2621440000 | tf_op jit(solution)/shard_map/project/pallas_call | solution.py:313
  81.4 2.9 collective-permute-done.1.rest_1_.rest_2_
  84.3 26.1 %attend_local.1 = (f32[256,2048]{1,0:T(8,128)}, f32[4,2048]{1,0:T(4,128)}) custom-call(s32[10]{0:T(128)} %pad_add_fusion.3.info, bf16[2048,256]{1,0:T(8,128)(2,1)} %get-tuple-element.93.q_ref, bf16[2048,512]{1,0:T(8,128)(2,1)} %get-tuple-element.71.k_ref.v_ref, bf16[2048,512]{1,0:T(8,128)(2,1)} %get-tuple-element.71.k_ref.v_ref), custom_call_target="tpu_custom_call" | custom-call | flops 2499999956992 | bytes 734003200 | tf_op jit(solution)/shard_map/attend_local/pallas_call | solution.py:607
  110.5 19.5 %attend_cross.1 = (bf16[128,2048]{1,0:T(8,128)(2,1)}, f32[2,2048]{1,0:T(2,128)}) custom-call(s32[10]{0:T(128)} %pad_add_fusion.3.info, bf16[2048,256]{1,0:T(8,128)(2,1)} %get-tuple-element.93.q_ref, bf16[2048,256]{1,0:T(8,128)(2,1)} %collective-permute-done.3.came_ref.came0.came1.came_q.came_do, ...), custom_call_target="tpu_custom_call" | custom-call | flops 1500000026624 | bytes 367001600 | tf_op jit(solution)/shard_map/attend_cross/pallas_call | solution.py:654
  130.0 3.9 collective-permute-start.4
  135.3 6.7 %collective-permute-done.5.lse_came = f32[2,2048]{1,0:T(2,128)S(1)} collective-permute-done((f32[2,2048]{1,0:T(2,128)}, f32[2,2048]{1,0:T(2,128)S(1)}, u32[]{:S(2)}, u32[]{:S(2)}) %collective-permute-start.5) | collective-permute-done | bytes 16416 | tf_op jit(solution)/shard_map/ppermute | solution.py:1009
  142.8 5.3 %merge.1 = (bf16[2048,256]{1,0:T(8,128)(2,1)}, f32[8,2048]{1,0:T(8,128)}) custom-call(s32[10]{0:T(128)} %pad_add_fusion.3.info, f32[256,2048]{1,0:T(8,128)} %get-tuple-element.74.local, f32[4,2048]{1,0:T(4,128)} %get-tuple-element.75.lse_local, bf16[128,2048]{1,0:T(8,128)(2,1)} %get-tuple-element.78.mine, f32[2,2048]{1,0:T(2,128)} %get-tuple-element.79.lse_mine, ...), custom_call_target="tpu_custom_call" | custom-call | flops 1048576000 | bytes 524288000 | tf_op jit(solution)/shard_map/merge/pallas_call | solution.py:698
  149.2 11.3 %collective-permute-start.7 = (f32[4,2048]{1,0:T(4,128)S(1)}, f32[4,2048]{1,0:T(4,128)S(1)}, u32[]{:S(2)}, u32[]{:S(2)}) collective-permute-start(f32[4,2048]{1,0:T(4,128)S(1)} %pad_maximum_fusion), channel_id=1, source_target_pairs={{8,0},{9,1},{10,2},{11,3},{12,4},{13,5},{14,6},{15,7},{24,16},{25,... | collective-permute-start | bytes 98312 | tf_op jit(solution)/shard_map/ppermute | solution.py:1024
  162.3 2.7 slice.143
  165.6 2.6 collective-permute-start.9
  168.2 27.1 %back_cross.1 = (f32[2048,128]{1,0:T(8,128)}, f32[2048,128]{1,0:T(8,128)}, f32[2048,128]{1,0:T(8,128)}, bf16[2048,256]{1,0:T(8,128)(2,1)}) custom-call(s32[10]{0:T(128)} %pad_add_fusion.3.info, bf16[2048,256]{1,0:T(8,128)(2,1)} %get-tuple-element.93.q_ref, bf16[2048,256]{1,0:T(8,128)(2,1)} %get-tuple-element.80.do_ref, ...), custom_call_target="tpu_custom_call" | custom-call | flops 2499999956992 | bytes 524288000 | tf_op jit(solution)/shard_map/back_cross/pallas_call | solution.py:879
  195.5 25.9 %hidden.1 = (bf16[2048,1024]{1,0:T(8,128)(2,1)}, bf16[2048,1024]{1,0:T(8,128)(2,1)}, f32[1,1024]{1,0:T(1,128)}) custom-call(s32[4]{0:T(128)} %pad_add_fusion.2.info, bf16[2048,2048]{1,0:T(8,128)(2,1)} %get-tuple-element.104.nrm.left_n.rest_7_, bf16[2048,2048]{1,0:T(8,128)(2,1)} %get-tuple-element.66.cot.left_c, bf16[1,1024]{1,0:T(2,128)(2,1)} %broadcast_in_dim.17.bias, ...), custom_call_target="tpu_custom_call" | custom-call | flops 1717986918400 | bytes 3355443200 | tf_op jit(solution)/shard_map/hidden/pallas_call | solution.py:349
  221.4 19.1 %branch.1 = bf16[1024,2048]{1,0:T(8,128)(2,1)} custom-call(bf16[2048,256]{1,0:T(8,128)(2,1)} %get-tuple-element.88.a.right_c, bf16[2048,1024]{1,0:T(8,128)(2,1)} %get-tuple-element.87.b.right_c, bf16[2048,1024]{1,0:T(8,128)(2,1)} %get-tuple-element.67.weights.rest_0_, bf16[512,2048]{1,0:T(8,128)(2,1)} %get-tuple-element.69.rest_0_.rest_1_, ...), custom_call_target="tpu_custom_call" | custom-call | flops 1073741824000 | bytes 1468006400 | tf_op jit(solution)/shard_map/branch/pallas_call | solution.py:418
  240.6 27.1 %hidden_grads.1 = (bf16[1024,1024]{1,0:T(8,128)(2,1)}, bf16[1024,1024]{1,0:T(8,128)(2,1)}, bf16[1024,1024]{1,0:T(8,128)(2,1)}, bf16[1024,1024]{1,0:T(8,128)(2,1)}) custom-call(s32[4]{0:T(128)} %pad_add_fusion.2.info, bf16[2048,2048]{1,0:T(8,128)(2,1)} %get-tuple-element.104.nrm.left_n.rest_7_, bf16[2048,2048]{1,0:T(8,128)(2,1)} %get-tuple-element.66.cot.left_c, ...), custom_call_target="tpu_custom_call" | custom-call | flops 1717986918400 | bytes 3355443200 | tf_op jit(solution)/shard_map/hidden_grads/pallas_call | solution.py:503
  271.1 41.8 %back_local.1 = (bf16[2048,768]{1,0:T(8,128)(2,1)}, f32[1,768]{1,0:T(1,128)}) custom-call(s32[10]{0:T(128)} %pad_add_fusion.3.info, bf16[2048,256]{1,0:T(8,128)(2,1)} %get-tuple-element.93.q_ref, bf16[2048,256]{1,0:T(8,128)(2,1)} %get-tuple-element.80.do_ref, f32[8,2048]{1,0:T(8,128)} %get-tuple-element.83.stat_ref, ...), custom_call_target="tpu_custom_call" | custom-call | flops 3999999983616 | bytes 1048576000 | tf_op jit(solution)/shard_map/back_local/pallas_call | solution.py:808
  316.9 25.6 %normed_grad.1 = (bf16[1024,2048]{1,0:T(8,128)(2,1)}, f32[1,2048]{1,0:T(1,128)}, f32[1,2048]{1,0:T(1,128)}) custom-call(bf16[2048,768]{1,0:T(8,128)(2,1)} %get-tuple-element.100.a.right_n, bf16[2048,1024]{1,0:T(8,128)(2,1)} %get-tuple-element.90.right_n.b, bf16[2048,1024]{1,0:T(8,128)(2,1)} %get-tuple-element.67.weights.rest_0_, ...), custom_call_target="tpu_custom_call" | custom-call | flops 1503238553600 | bytes 1887436800 | tf_op jit(solution)/shard_map/normed_grad/pallas_call | solution.py:418
  343.7 2.6 add_convert_fusion.1
  348.4 2.6 add_convert_fusion
  353.0 16.6 %collective-permute-done.16 = f32[1,7936]{1,0:T(1,128)S(1)} collective-permute-done((f32[1,7936]{1,0:T(1,128)S(1)}, f32[1,7936]{1,0:T(1,128)S(1)}, u32[]{:S(2)}, u32[]{:S(2)}) %collective-permute-start.16) | collective-permute-done | bytes 31776 | tf_op jit(solution)/shard_map/ppermute | solution.py:970
  370.2 19.2 %packed_grads.1 = (bf16[1024,768]{1,0:T(8,128)(2,1)}, bf16[1024,768]{1,0:T(8,128)(2,1)}, bf16[1024,256]{1,0:T(8,128)(2,1)}, bf16[1024,256]{1,0:T(8,128)(2,1)}) custom-call(s32[4]{0:T(128)} %pad_add_fusion.2.info, bf16[2048,2048]{1,0:T(8,128)(2,1)} %get-tuple-element.104.nrm.left_n.rest_7_, bf16[2048,2048]{1,0:T(8,128)(2,1)} %get-tuple-element.66.cot.left_c, ...), custom_call_target="tpu_custom_call" | custom-call | flops 858993459200 | bytes 2516582400 | tf_op jit(solution)/shard_map/packed_grads/pallas_call | solution.py:503
  398.0 2.6 collective-permute-done.18
  400.7 2.3 collective-permute-start.19
  404.1 3.2 collective-permute-done.19
  407.4 3.6 layer_out.1
  411.0 2.2 convert_add_fusion.1
  418.7 2.5 fusion
  423.1 2.9 copy.33
  431.1 2.4 collective-permute-done.26
  434.7 13.8 %collective-permute-done.23 = bf16[512,768]{1,0:T(8,128)(2,1)S(1)} collective-permute-done((bf16[512,768]{1,0:T(8,128)(2,1)S(1)}, bf16[512,768]{1,0:T(8,128)(2,1)S(1)}, u32[]{:S(2)}, u32[]{:S(2)}) %collective-permute-start.23) | collective-permute-done | bytes 786464 | tf_op jit(solution)/shard_map/ppermute | solution.py:970
  457.6 5.4 %input_grad.1 = bf16[256,2048]{1,0:T(8,128)(2,1)} custom-call(s32[4]{0:T(128)} %pad_add_fusion.2.info, bf16[256,2048]{1,0:T(8,128)(2,1)} %reduce-scatter.5.cloned.1.call-done.grad, bf16[1024,2048]{1,0:T(8,128)(2,1)} %tok.5, bf16[1024,2048]{1,0:T(8,128)(2,1)} %cot.3, bf16[1,2048]{1,0:T(2,128)(2,1)} %broadcast_in_dim.19.gain), custom_call_target="tpu_custom_call" | custom-call | flops 1048576000 | bytes 419430400 | tf_op jit(solution)/shard_map/input_grad/pallas_call | solution.py:921
  (171 shorter events, 60.1 us)
Async XLA Ops:
  7.2 51.6 %copy-start = (bf16[3,512]{1,0:T(4,128)(2,1)S(1)}, bf16[3,512]{1,0:T(4,128)(2,1)}, u32[]{:S(2)}) copy-start(bf16[3,512]{1,0:T(4,128)(2,1)} %param.20) | copy-start | bytes 9220
  7.2 400.2 %reduce-scatter.3.cloned.1.call-start = ((), (), s32[]{:S(2)}) async-start(), calls=%async_computation.2 | async-start | bytes 5242880 | tf_op jit(solution)/shard_map/reduce_scatter | solution.py:1048
  8.0 51.9 %collective-permute-start = (s32[2,1024]{1,0:T(2,128)S(1)}, s32[2,1024]{1,0:T(2,128)S(1)}, u32[]{:S(2)}, u32[]{:S(2)}) collective-permute-start(s32[2,1024]{1,0:T(2,128)S(1)} %pad_add_fusion.1), channel_id=1, source_target_pairs={{0,4},{4,0},{1,5},{5,1},{2,6},{6,2},{3,7},{7,3},{8,12},{12,8},{9,1... | collective-permute-start | bytes 24584 | tf_op jit(solution)/shard_map/ppermute | solution.py:968
  53.5 108.8 %collective-permute-start.8 = (bf16[512,2048]{1,0:T(8,128)(2,1)}, bf16[512,2048]{1,0:T(8,128)(2,1)}, u32[]{:S(2)}, u32[]{:S(2)}) collective-permute-start(bf16[512,2048]{1,0:T(8,128)(2,1)} %get-tuple-element.69.rest_0_.rest_1_), channel_id=1, source_target_pairs={{0,16},{16,0},{1,17},{17,1},{2,18},{18,2},{3,19},{19,3},{4,20},{20... | collective-permute-start | bytes 6291464 | tf_op jit(solution)/shard_map/ppermute | solution.py:970
  58.2 26.1 %collective-permute-start.1 = (bf16[256,2048]{1,0:T(8,128)(2,1)}, bf16[256,2048]{1,0:T(8,128)(2,1)}, u32[]{:S(2)}, u32[]{:S(2)}) collective-permute-start(bf16[256,2048]{1,0:T(8,128)(2,1)} %get-tuple-element.146), channel_id=1, source_target_pairs={{0,8},{8,0},{1,9},{9,1},{2,10},{10,2},{3,11},{11,3},{4,12},{12,4},... | collective-permute-start | bytes 3145736 | tf_op jit(solution)/shard_map/ppermute | solution.py:969
  79.1 31.4 %collective-permute-start.3 = (bf16[2048,256]{1,0:T(8,128)(2,1)}, bf16[2048,256]{1,0:T(8,128)(2,1)}, u32[]{:S(2)}, u32[]{:S(2)}) collective-permute-start(bf16[2048,256]{1,0:T(8,128)(2,1)} %get-tuple-element.77), channel_id=1, source_target_pairs={{0,8},{8,0},{1,9},{9,1},{2,10},{10,2},{3,11},{11,3},{4,12},{12,4},... | collective-permute-start | bytes 3145736 | tf_op jit(solution)/shard_map/ppermute | solution.py:969
  110.4 24.9 %collective-permute-start.2 = (bf16[256,2048]{1,0:T(8,128)(2,1)}, bf16[256,2048]{1,0:T(8,128)(2,1)}, u32[]{:S(2)}, u32[]{:S(2)}) collective-permute-start(bf16[256,2048]{1,0:T(8,128)(2,1)} %get-tuple-element.73), channel_id=1, source_target_pairs={{0,8},{8,0},{1,9},{9,1},{2,10},{10,2},{3,11},{11,3},{4,12},{12,4},... | collective-permute-start | bytes 3145736 | tf_op jit(solution)/shard_map/ppermute | solution.py:969
  130.0 12.0 %collective-permute-start.4 = (bf16[128,2048]{1,0:T(8,128)(2,1)}, bf16[128,2048]{1,0:T(8,128)(2,1)S(1)}, u32[]{:S(2)}, u32[]{:S(2)}) collective-permute-start(bf16[128,2048]{1,0:T(8,128)(2,1)} %get-tuple-element.78.mine), channel_id=1, source_target_pairs={{0,8},{1,9},{2,10},{3,11},{4,12},{5,13},{6,14},{7,15},{16,24},{17,... | collective-permute-start | bytes 1572872 | tf_op jit(solution)/shard_map/ppermute | solution.py:1009
  133.9 28.3 %collective-permute-start.6 = (bf16[256,2048]{1,0:T(8,128)(2,1)}, bf16[256,2048]{1,0:T(8,128)(2,1)S(1)}, u32[]{:S(2)}, u32[]{:S(2)}) collective-permute-start(bf16[256,2048]{1,0:T(8,128)(2,1)} %collective-permute-done.1.rest_1_.rest_2_), channel_id=1, source_target_pairs={{0,16},{16,0},{1,17},{17,1},{2,18},{18,2},{3,19},{19,3},{4,20},{20... | collective-permute-start | bytes 3145736 | tf_op jit(solution)/shard_map/ppermute | solution.py:970
  134.0 8.0 %collective-permute-start.5 = (f32[2,2048]{1,0:T(2,128)}, f32[2,2048]{1,0:T(2,128)S(1)}, u32[]{:S(2)}, u32[]{:S(2)}) collective-permute-start(f32[2,2048]{1,0:T(2,128)} %get-tuple-element.79.lse_mine), channel_id=1, source_target_pairs={{0,8},{1,9},{2,10},{3,11},{4,12},{5,13},{6,14},{7,15},{16,24},{17,... | collective-permute-start | bytes 49160 | tf_op jit(solution)/shard_map/ppermute | solution.py:1009
  149.2 15.8 %collective-permute-start.7 = (f32[4,2048]{1,0:T(4,128)S(1)}, f32[4,2048]{1,0:T(4,128)S(1)}, u32[]{:S(2)}, u32[]{:S(2)}) collective-permute-start(f32[4,2048]{1,0:T(4,128)S(1)} %pad_maximum_fusion), channel_id=1, source_target_pairs={{8,0},{9,1},{10,2},{11,3},{12,4},{13,5},{14,6},{15,7},{24,16},{25,... | collective-permute-start | bytes 98312 | tf_op jit(solution)/shard_map/ppermute | solution.py:1024
  165.6 29.9 %collective-permute-start.9 = (bf16[256,2048]{1,0:T(8,128)(2,1)}, bf16[256,2048]{1,0:T(8,128)(2,1)}, u32[]{:S(2)}, u32[]{:S(2)}) collective-permute-start(bf16[256,2048]{1,0:T(8,128)(2,1)} %slice.143), channel_id=1, source_target_pairs={{0,8},{8,0},{1,9},{9,1},{2,10},{10,2},{3,11},{11,3},{4,12},{12,4},... | collective-permute-start | bytes 3145736 | tf_op jit(solution)/shard_map/ppermute | solution.py:969
  195.4 75.7 %collective-permute-start.10 = (bf16[2048,256]{1,0:T(8,128)(2,1)}, bf16[2048,256]{1,0:T(8,128)(2,1)}, u32[]{:S(2)}, u32[]{:S(2)}) collective-permute-start(bf16[2048,256]{1,0:T(8,128)(2,1)} %get-tuple-element.84), channel_id=1, source_target_pairs={{0,8},{8,0},{1,9},{9,1},{2,10},{10,2},{3,11},{11,3},{4,12},{12,4},... | collective-permute-start | bytes 3145736 | tf_op jit(solution)/shard_map/ppermute | solution.py:969
  240.6 217.0 %reduce-scatter.5.cloned.1.call-start = ((), (), s32[]{:S(2)}) async-start(), calls=%async_computation.3 | async-start | bytes 5242880 | tf_op jit(solution)/shard_map/reduce_scatter | solution.py:1058
  267.7 49.1 %collective-permute-start.11 = (bf16[1024,1024]{1,0:T(8,128)(2,1)}, bf16[1024,1024]{1,0:T(8,128)(2,1)}, u32[]{:S(2)}, u32[]{:S(2)}) collective-permute-start(bf16[1024,1024]{1,0:T(8,128)(2,1)} %get-tuple-element.98), channel_id=1, source_target_pairs={{0,8},{8,0},{1,9},{9,1},{2,10},{10,2},{3,11},{11,3},{4,12},{12,4},... | collective-permute-start | bytes 6291464 | tf_op jit(solution)/shard_map/ppermute | solution.py:969
  269.8 47.0 %collective-permute-start.12 = (bf16[1024,1024]{1,0:T(8,128)(2,1)}, bf16[1024,1024]{1,0:T(8,128)(2,1)}, u32[]{:S(2)}, u32[]{:S(2)}) collective-permute-start(bf16[1024,1024]{1,0:T(8,128)(2,1)} %get-tuple-element.99), channel_id=1, source_target_pairs={{0,16},{16,0},{1,17},{17,1},{2,18},{18,2},{3,19},{19,3},{4,20},{20... | collective-permute-start | bytes 6291464 | tf_op jit(solution)/shard_map/ppermute | solution.py:970
  271.1 41.8 %copy-start.8 = (bf16[1024,1024]{1,0:T(8,128)(2,1)S(1)}, bf16[1024,1024]{1,0:T(8,128)(2,1)}, u32[]{:S(2)}) copy-start(bf16[1024,1024]{1,0:T(8,128)(2,1)} %get-tuple-element.92) | copy-start | bytes 6291460
  343.5 4.0 collective-permute-start.15
  346.3 61.1 %collective-permute-start.13 = (bf16[512,1024]{1,0:T(8,128)(2,1)}, bf16[512,1024]{1,0:T(8,128)(2,1)}, u32[]{:S(2)}, u32[]{:S(2)}) collective-permute-start(bf16[512,1024]{1,0:T(8,128)(2,1)} %add_convert_fusion.1), channel_id=1, source_target_pairs={{0,16},{16,0},{1,17},{17,1},{2,18},{18,2},{3,19},{19,3},{4,20},{20... | collective-permute-start | bytes 3145736 | tf_op jit(solution)/shard_map/ppermute | solution.py:970
  347.5 22.1 %collective-permute-start.16 = (f32[1,7936]{1,0:T(1,128)S(1)}, f32[1,7936]{1,0:T(1,128)S(1)}, u32[]{:S(2)}, u32[]{:S(2)}) collective-permute-start(f32[1,7936]{1,0:T(1,128)S(1)} %add.99), channel_id=1, source_target_pairs={{0,16},{16,0},{1,17},{17,1},{2,18},{18,2},{3,19},{19,3},{4,20},{20... | collective-permute-start | bytes 95240 | tf_op jit(solution)/shard_map/ppermute | solution.py:970
  351.0 56.3 %collective-permute-start.14 = (bf16[512,1024]{1,0:T(8,128)(2,1)}, bf16[512,1024]{1,0:T(8,128)(2,1)}, u32[]{:S(2)}, u32[]{:S(2)}) collective-permute-start(bf16[512,1024]{1,0:T(8,128)(2,1)} %add_convert_fusion), channel_id=1, source_target_pairs={{0,8},{8,0},{1,9},{9,1},{2,10},{10,2},{3,11},{11,3},{4,12},{12,4},... | collective-permute-start | bytes 3145736 | tf_op jit(solution)/shard_map/ppermute | solution.py:969
  370.2 24.6 %collective-permute-start.17 = (f32[1,7936]{1,0:T(1,128)}, f32[1,7936]{1,0:T(1,128)}, u32[]{:S(2)}, u32[]{:S(2)}) collective-permute-start(f32[1,7936]{1,0:T(1,128)} %add.100), channel_id=1, source_target_pairs={{0,4},{4,0},{1,5},{5,1},{2,6},{6,2},{3,7},{7,3},{8,12},{12,8},{9,1... | collective-permute-start | bytes 95240 | tf_op jit(solution)/shard_map/ppermute | solution.py:968
  390.6 37.6 %collective-permute-start.20 = (bf16[1024,768]{1,0:T(8,128)(2,1)}, bf16[1024,768]{1,0:T(8,128)(2,1)}, u32[]{:S(2)}, u32[]{:S(2)}) collective-permute-start(bf16[1024,768]{1,0:T(8,128)(2,1)} %get-tuple-element.105), channel_id=1, source_target_pairs={{0,8},{8,0},{1,9},{9,1},{2,10},{10,2},{3,11},{11,3},{4,12},{12,4},... | collective-permute-start | bytes 4718600 | tf_op jit(solution)/shard_map/ppermute | solution.py:969
  393.4 22.7 %collective-permute-start.25 = (bf16[1024,256]{1,0:T(8,128)(2,1)}, bf16[1024,256]{1,0:T(8,128)(2,1)S(1)}, u32[]{:S(2)}, u32[]{:S(2)}) collective-permute-start(bf16[1024,256]{1,0:T(8,128)(2,1)} %get-tuple-element.117), channel_id=1, source_target_pairs={{0,16},{16,0},{1,17},{17,1},{2,18},{18,2},{3,19},{19,3},{4,20},{20... | collective-permute-start | bytes 1572872 | tf_op jit(solution)/shard_map/ppermute | solution.py:970
  395.7 5.0 %collective-permute-start.18 = (f32[1,6144]{1,0:T(1,128)S(1)}, f32[1,6144]{1,0:T(1,128)S(1)}, u32[]{:S(2)}, u32[]{:S(2)}) collective-permute-start(f32[1,6144]{1,0:T(1,128)S(1)} %slice_add_fusion), channel_id=1, source_target_pairs={{0,1},{1,0},{2,3},{3,2},{4,5},{5,4},{6,7},{7,6},{8,9},{9,8},{10,11... | collective-permute-start | bytes 73736 | tf_op jit(solution)/shard_map/ppermute | solution.py:1124
  400.7 6.6 %collective-permute-start.19 = (f32[1,6144]{1,0:T(1,128)S(1)}, f32[1,6144]{1,0:T(1,128)S(1)}, u32[]{:S(2)}, u32[]{:S(2)}) collective-permute-start(f32[1,6144]{1,0:T(1,128)S(1)} %add.102), channel_id=1, source_target_pairs={{0,2},{1,3},{2,0},{3,1},{4,6},{5,7},{6,4},{7,5},{8,10},{9,11},{10,... | collective-permute-start | bytes 73736 | tf_op jit(solution)/shard_map/ppermute | solution.py:1124
  413.3 5.2 %collective-permute-start.21 = (bf16[256,1024]{1,0:T(8,128)(2,1)S(1)}, bf16[256,1024]{1,0:T(8,128)(2,1)S(1)}, u32[]{:S(2)}, u32[]{:S(2)}) collective-permute-start(bf16[256,1024]{1,0:T(8,128)(2,1)S(1)} %dynamic-slice_convert_fusion.1), channel_id=1, source_target_pairs={{0,4},{4,0},{1,5},{5,1},{2,6},{6,2},{3,7},{7,3},{8,12},{12,8},{9,1... | collective-permute-start | bytes 1572872 | tf_op jit(solution)/shard_map/ppermute | solution.py:968
  415.6 3.0 collective-permute-start.22
  416.8 16.7 %collective-permute-start.26 = (bf16[512,256]{1,0:T(8,128)(2,1)}, bf16[512,256]{1,0:T(8,128)(2,1)}, u32[]{:S(2)}, u32[]{:S(2)}) collective-permute-start(bf16[512,256]{1,0:T(8,128)(2,1)} %add_convert_fusion.3), channel_id=1, source_target_pairs={{0,8},{8,0},{1,9},{9,1},{2,10},{10,2},{3,11},{11,3},{4,12},{12,4},... | collective-permute-start | bytes 786440 | tf_op jit(solution)/shard_map/ppermute | solution.py:969
  429.5 19.0 %collective-permute-start.23 = (bf16[512,768]{1,0:T(8,128)(2,1)S(1)}, bf16[512,768]{1,0:T(8,128)(2,1)S(1)}, u32[]{:S(2)}, u32[]{:S(2)}) collective-permute-start(bf16[512,768]{1,0:T(8,128)(2,1)S(1)} %add_convert_fusion.2), channel_id=1, source_target_pairs={{0,16},{16,0},{1,17},{17,1},{2,18},{18,2},{3,19},{19,3},{4,20},{20... | collective-permute-start | bytes 2359304 | tf_op jit(solution)/shard_map/ppermute | solution.py:970
  434.6 16.6 %collective-permute-start.27 = (bf16[256,256]{1,0:T(8,128)(2,1)S(1)}, bf16[256,256]{1,0:T(8,128)(2,1)S(1)}, u32[]{:S(2)}, u32[]{:S(2)}) collective-permute-start(bf16[256,256]{1,0:T(8,128)(2,1)S(1)} %dynamic-slice_convert_fusion.3), channel_id=1, source_target_pairs={{0,4},{4,0},{1,5},{5,1},{2,6},{6,2},{3,7},{7,3},{8,12},{12,8},{9,1... | collective-permute-start | bytes 393224 | tf_op jit(solution)/shard_map/ppermute | solution.py:968
  451.1 4.4 collective-permute-start.24
  (23 other events, 330.2 us)
Sparse Core Ops, SparseCore 0:
  240.7 78.2 reduce-scatter.2
  353.1 77.3 reduce-scatter.4
